TPU v7x, 32 devices: a whole 2x2x4 slice. The times are simulated.
32 devices in a mesh: dp: 4 (over y, core), tm: 8 (over z, x).
Axes of the slice: x: 2, y: 2, z: 4, core: 2. Of those that a mesh axis runs over, the one named last changes fastest.
Arguments:
- inputs: bfloat16 [16, 2048, 1024], P('dp', 'tm'), may hold values from -6 to 6
- cotangent: bfloat16 [16, 2048, 1024], P('dp', 'tm'), may hold values from -6 to 6
- lengths: int32 [16], P('dp'), may hold values from 512 to 2048, as said below
- first_up: bfloat16 [1024, 4096], P('tm'), may hold values from -0.1875 to 0.1875
- first_down: bfloat16 [4096, 1024], P('tm'), may hold values from -0.09375 to 0.09375
- joint_proj: bfloat16 [1024, 3072], P('tm'), may hold values from -0.1875 to 0.1875
- rel_proj: bfloat16 [1024, 1024], P('tm'), may hold values from -0.1875 to 0.1875
- merge_proj: bfloat16 [1024, 1024], P('tm'), may hold values from -2 to 2
- conv_wide: bfloat16 [1024, 2048], P('tm'), may hold values from -0.1875 to 0.1875
- conv_narrow: bfloat16 [1024, 1024], P('tm'), may hold values from -0.1875 to 0.1875
- second_up: bfloat16 [1024, 4096], P('tm'), may hold values from -0.1875 to 0.1875
- second_down: bfloat16 [4096, 1024], P('tm'), may hold values from -0.09375 to 0.09375
- norm_gains: bfloat16 [6, 1024], P(None, 'tm'), may hold values from 0.5 to 1.5
- norm_shifts: bfloat16 [6, 1024], P(None, 'tm'), may hold values from -1 to 1
- pos_biases: bfloat16 [2, 1024], P(None, 'tm'), may hold values from -3 to 3
- depth_taps: bfloat16 [5, 1024], P(None, 'tm'), may hold values from -2.5 to 2.5
Outputs:
- output: bfloat16 [16, 2048, 1024], P('dp', 'tm')
- grad_inputs: bfloat16 [16, 2048, 1024], P('dp', 'tm')
- grad_first_up: float32 [1024, 4096], P('tm')
- grad_first_down: float32 [4096, 1024], P('tm')
- grad_joint_proj: float32 [1024, 3072], P('tm')
- grad_rel_proj: float32 [1024, 1024], P('tm')
- grad_merge_proj: float32 [1024, 1024], P('tm')
- grad_conv_wide: float32 [1024, 2048], P('tm')
- grad_conv_narrow: float32 [1024, 1024], P('tm')
- grad_second_up: float32 [1024, 4096], P('tm')
- grad_second_down: float32 [4096, 1024], P('tm')
- grad_norm_gains: float32 [6, 1024], P(None, 'tm')
- grad_norm_shifts: float32 [6, 1024], P(None, 'tm')
- grad_pos_biases: float32 [2, 1024], P(None, 'tm')
- grad_depth_taps: float32 [5, 1024], P(None, 'tm')
Inputs may be any that keep to these rules, and one draw needn't show every extreme that they name: `lengths`: in each group of 4 consecutive utterances the longest possible length grows with the group's index; the first utterance has 512 frames and the last 2048.
All inputs are finite; a program needn't handle non-finite values.
Results may differ from a plain program's by a relative error of at most 0.024.
Values may be sent and summed in bfloat16 or wider, within the bound.
No kernel may reach another device: no remote copies, remote signals or barrier semaphores. Data moves between devices by JAX's collectives and lax.ppermute only.
A program may use at most 384 MiB of HBM per device.

v0:
```python
import math

import jax
import jax.numpy as jnp
from jax import lax
from jax.sharding import PartitionSpec as P

D = 1024
HEADS = 8
HEAD_DIM = 128
KW = 5


eps_norm = 1e-05
neg_fill = -1e30


def padded_2(shard, sides, width):
    for axis, dim in sides:
        size, length = (lax.axis_size(axis), shard.shape[dim])
        up = [(i, (i + 1) % size) for i in range(size - 1)]
        down = [(j, i) for i, j in up]
        last = lax.slice_in_dim(shard, length - width, length, axis=dim)
        leading = lax.slice_in_dim(shard, 0, width, axis=dim)
        before = lax.ppermute(last, axis, up)
        after = lax.ppermute(leading, axis, down)
        shard = jnp.concatenate([before, shard, after], axis=dim)
    return shard


def product(left, right):
    return jnp.dot(left, right, preferred_element_type=jnp.float32)


def product_nt(left, right):
    return lax.dot_general(
        left, right, (((1,), (1,)), ((), ())), preferred_element_type=jnp.float32
    )


def product_tn(left, right):
    return lax.dot_general(
        left, right, (((0,), (0,)), ((), ())), preferred_element_type=jnp.float32
    )


def norm_fwd(values, gain_row, shift_row):
    centered = values - jnp.mean(values, axis=-1, keepdims=True)
    scale_inv = lax.rsqrt(jnp.mean(centered * centered, axis=-1, keepdims=True) + eps_norm)
    normal = centered * scale_inv
    return (normal * gain_row + shift_row, normal, scale_inv)


def norm_back(grad_out, normal, scale_inv, gain_row):
    grad_norm = grad_out * gain_row
    grad_in = scale_inv * (
        grad_norm
        - jnp.mean(grad_norm, axis=-1, keepdims=True)
        - normal * jnp.mean(grad_norm * normal, axis=-1, keepdims=True)
    )
    return (grad_in, jnp.sum(grad_out * normal, axis=0), jnp.sum(grad_out, axis=0))


def swish_grad(values):
    sigmoid_val = jax.nn.sigmoid(values)
    return sigmoid_val * (1.0 + values * (1.0 - sigmoid_val))


def sinusoid(distance, feat_width):
    half_width = feat_width // 2
    inv_freq = jnp.exp(
        jnp.arange(half_width, dtype=jnp.float32) * (-2.0 * math.log(10000.0) / feat_width)
    )
    angles = distance[:, None] * inv_freq[None, :]
    return jnp.concatenate([jnp.sin(angles), jnp.cos(angles)], axis=1)


def rel_shift(raw, key_count):
    lead_dims = raw.shape[:-2]
    row_count = raw.shape[-2]
    col_span = raw.shape[-1]
    flattened = raw.reshape(lead_dims + (row_count * col_span,))
    flattened = flattened[..., row_count - 1 : row_count - 1 + row_count * (col_span - 1)]
    return flattened.reshape(lead_dims + (row_count, col_span - 1))[..., :key_count]


def rel_unshift(grad, col_span):
    lead_count, row_count, key_count = grad.shape
    padded = jnp.pad(grad, ((0, 0), (0, 0), (0, col_span - 1 - key_count)))
    flattened = padded.reshape(lead_count, row_count * (col_span - 1))
    flattened = jnp.pad(flattened, ((0, 0), (row_count - 1, 1)))
    return flattened.reshape(lead_count, row_count, col_span)


def feed_forward(values, gain_row, shift_row, up_weight, down_weight):
    normed, normal, scale_inv = norm_fwd(values, gain_row, shift_row)
    normed_low = normed.astype(jnp.bfloat16)
    hidden = product(normed_low, up_weight)
    active_low = (hidden * jax.nn.sigmoid(hidden)).astype(jnp.bfloat16)
    return (product(active_low, down_weight), (normal, scale_inv, normed_low, hidden, active_low))


def feed_back(grad_result, saved_acts, gain_row, up_weight, down_weight):
    normal, scale_inv, normed_low, hidden, active_low = saved_acts
    grad_low = grad_result.astype(jnp.bfloat16)
    grad_down = product_tn(active_low, grad_low)
    grad_hidden = (product_nt(grad_low, down_weight) * swish_grad(hidden)).astype(jnp.bfloat16)
    grad_up = product_tn(normed_low, grad_hidden)
    grad_values, grad_gain, grad_shift = norm_back(
        product_nt(grad_hidden, up_weight), normal, scale_inv, gain_row
    )
    return (grad_values, grad_up, grad_down, grad_gain, grad_shift)


def body(
    inputs,
    cotangent,
    lengths,
    first_up,
    first_down,
    joint_proj,
    rel_proj,
    merge_proj,
    conv_wide,
    conv_narrow,
    second_up,
    second_down,
    norm_gains,
    norm_shifts,
    pos_biases,
    depth_taps,
):
    (
        up_one,
        down_one,
        joint_full,
        rel_full,
        merge_full,
        wide_full,
        narrow_full,
        up_two,
        down_two,
        gain_low,
        shift_low,
        bias_low,
        taps_low,
    ) = (
        lax.all_gather(first_up, "tm", axis=0, tiled=True),
        lax.all_gather(first_down, "tm", axis=0, tiled=True),
        lax.all_gather(joint_proj, "tm", axis=0, tiled=True),
        lax.all_gather(rel_proj, "tm", axis=0, tiled=True),
        lax.all_gather(merge_proj, "tm", axis=0, tiled=True),
        lax.all_gather(conv_wide, "tm", axis=0, tiled=True),
        lax.all_gather(conv_narrow, "tm", axis=0, tiled=True),
        lax.all_gather(second_up, "tm", axis=0, tiled=True),
        lax.all_gather(second_down, "tm", axis=0, tiled=True),
        lax.all_gather(norm_gains, "tm", axis=1, tiled=True),
        lax.all_gather(norm_shifts, "tm", axis=1, tiled=True),
        lax.all_gather(pos_biases, "tm", axis=1, tiled=True),
        lax.all_gather(depth_taps, "tm", axis=1, tiled=True),
    )
    gain_rows = gain_low.astype(jnp.float32)
    shift_rows = shift_low.astype(jnp.float32)
    bias_rows = bias_low.astype(jnp.float32)
    kernel_taps = taps_low.astype(jnp.float32)
    time_devs = lax.axis_size("tm")
    time_index = lax.axis_index("tm")
    utt_count, stretch_len, feat_width = inputs.shape
    slot_len = stretch_len * time_devs
    row_count = utt_count * stretch_len
    rel_span = stretch_len + slot_len - 1
    pad_width = KW // 2
    score_scale = HEAD_DIM ** (-0.5)
    frame_pos = time_index * stretch_len + jnp.arange(stretch_len, dtype=jnp.int32)
    live_col = (frame_pos[None, :] < lengths[:, None]).astype(jnp.float32)[:, :, None]
    key_live = jnp.arange(slot_len, dtype=jnp.int32)[None, :] < lengths[:, None]
    section_zero = inputs.astype(jnp.float32).reshape(row_count, feat_width)

    def to_heads(values):
        return values.reshape(utt_count, stretch_len, HEADS, HEAD_DIM).transpose(2, 0, 1, 3)

    def from_heads(values):
        return values.transpose(1, 2, 0, 3).reshape(row_count, D)

    def scores_for(query_u, query_v, keys_all, rel_head):
        content = jnp.einsum("uqc,ukc->uqk", query_u, keys_all, preferred_element_type=jnp.float32)
        raw_rel = jnp.einsum("uqc,wc->uqw", query_v, rel_head, preferred_element_type=jnp.float32)
        scores = (content + rel_shift(raw_rel, slot_len)) * score_scale
        return jnp.where(key_live[:, None, :], scores, neg_fill)

    def head_forward(mapped):
        query_u, query_v, key_part, value_part, rel_head = mapped
        keys_all, values_all = (
            lax.all_gather(key_part, "tm", axis=1, tiled=True),
            lax.all_gather(value_part, "tm", axis=1, tiled=True),
        )
        masked = scores_for(query_u, query_v, keys_all, rel_head)
        row_max = jnp.max(masked, axis=-1, keepdims=True)
        exp_scores = jnp.exp(masked - row_max)
        exp_total = jnp.sum(exp_scores, axis=-1, keepdims=True)
        probs_low = (exp_scores / exp_total).astype(jnp.bfloat16)
        mixed = jnp.einsum(
            "uqk,ukc->uqc", probs_low, values_all, preferred_element_type=jnp.float32
        )
        log_total = row_max[..., 0] + jnp.log(exp_total[..., 0])
        return (mixed, log_total, key_part, value_part)

    def head_backward(mapped):
        query_u, query_v, key_src, value_src, rel_head, log_total, grad_out = mapped
        keys_all, values_all = (
            lax.all_gather(key_src, "tm", axis=1, tiled=True),
            lax.all_gather(value_src, "tm", axis=1, tiled=True),
        )
        masked = scores_for(query_u, query_v, keys_all, rel_head)
        prob_full = jnp.exp(masked - log_total[..., None])
        grad_prob = jnp.einsum(
            "uqc,ukc->uqk", grad_out, values_all, preferred_element_type=jnp.float32
        )
        grad_values = jnp.einsum(
            "uqk,uqc->ukc",
            prob_full.astype(jnp.bfloat16),
            grad_out,
            preferred_element_type=jnp.float32,
        )
        inner_sum = jnp.sum(prob_full * grad_prob, axis=-1, keepdims=True)
        grad_scores = (prob_full * (grad_prob - inner_sum)).astype(jnp.bfloat16)
        grad_query_u = (
            jnp.einsum("uqk,ukc->uqc", grad_scores, keys_all, preferred_element_type=jnp.float32)
            * score_scale
        )
        grad_keys = (
            jnp.einsum("uqk,uqc->ukc", grad_scores, query_u, preferred_element_type=jnp.float32)
            * score_scale
        )
        grad_raw = rel_unshift(grad_scores, rel_span)
        grad_query_v = (
            jnp.einsum("uqw,wc->uqc", grad_raw, rel_head, preferred_element_type=jnp.float32)
            * score_scale
        )
        grad_rel = (
            jnp.einsum("uqw,uqc->wc", grad_raw, query_v, preferred_element_type=jnp.float32)
            * score_scale
        )
        keys_own, values_own = (
            lax.psum_scatter(
                grad_keys.astype(jnp.bfloat16), "tm", scatter_dimension=1, tiled=True
            ).astype(jnp.float32),
            lax.psum_scatter(
                grad_values.astype(jnp.bfloat16), "tm", scatter_dimension=1, tiled=True
            ).astype(jnp.float32),
        )
        return (grad_query_u, grad_query_v, keys_own, values_own, grad_rel)

    branch_one, saved_one = feed_forward(
        section_zero, gain_rows[0], shift_rows[0], up_one, down_one
    )
    section_one = section_zero + 0.5 * branch_one
    att_normed, att_normal, att_inv = norm_fwd(section_one, gain_rows[1], shift_rows[1])
    att_low = att_normed.astype(jnp.bfloat16)
    joint_out = product(att_low, joint_full)
    query = joint_out[:, :D]
    query_u = (query + bias_rows[0]).astype(jnp.bfloat16)
    query_v = (query + bias_rows[1]).astype(jnp.bfloat16)
    key_low = joint_out[:, D : 2 * D].astype(jnp.bfloat16)
    value_low = joint_out[:, 2 * D :].astype(jnp.bfloat16)
    distance = ((time_index + 1) * stretch_len - 1 - jnp.arange(rel_span, dtype=jnp.int32)).astype(
        jnp.float32
    )
    table_low = sinusoid(distance, D).astype(jnp.bfloat16)
    rel_low = product(table_low, rel_full).astype(jnp.bfloat16)
    rel_heads = rel_low.reshape(rel_span, HEADS, HEAD_DIM).transpose(1, 0, 2)
    heads_u = to_heads(query_u)
    heads_v = to_heads(query_v)
    mixed_heads, log_totals, key_store, value_store = lax.map(
        head_forward, (heads_u, heads_v, to_heads(key_low), to_heads(value_low), rel_heads)
    )
    attended_low = from_heads(mixed_heads).astype(jnp.bfloat16)
    section_two = section_one + product(attended_low, merge_full)
    conv_normed, conv_normal, conv_inv = norm_fwd(section_two, gain_rows[2], shift_rows[2])
    conv_low = conv_normed.astype(jnp.bfloat16)
    wide_out = product(conv_low, wide_full)
    lin_half = wide_out[:, :D]
    gate_sig = jax.nn.sigmoid(wide_out[:, D:])
    gated = (lin_half * gate_sig).reshape(utt_count, stretch_len, D) * live_col
    framed = padded_2(gated.astype(jnp.bfloat16), (("tm", 1),), pad_width).astype(gated.dtype)
    depth_out = kernel_taps[0] * framed[:, 0:stretch_len]
    for offset in range(1, KW):
        depth_out = depth_out + kernel_taps[offset] * framed[:, offset : offset + stretch_len]
    local_count = jnp.sum(live_col)
    local_sum = jnp.sum(depth_out * live_col, axis=(0, 1))
    total_sum, total_count = lax.psum((local_sum, local_count), ("dp", "tm"))
    bn_mean = total_sum / total_count
    centered = depth_out - bn_mean
    total_var = lax.psum(jnp.sum(centered * centered * live_col, axis=(0, 1)), ("dp", "tm"))
    variance = total_var / total_count
    bn_inv = lax.rsqrt(variance + eps_norm)
    bn_normal = centered * bn_inv
    bn_flat = (bn_normal * gain_rows[5] + shift_rows[5]).reshape(row_count, D)
    swish_low = (bn_flat * jax.nn.sigmoid(bn_flat)).astype(jnp.bfloat16)
    section_three = section_two + product(swish_low, narrow_full)
    branch_four, saved_four = feed_forward(
        section_three, gain_rows[3], shift_rows[3], up_two, down_two
    )
    section_four = section_three + 0.5 * branch_four
    final_out, final_normal, final_inv = norm_fwd(section_four, gain_rows[4], shift_rows[4])
    grad_final = cotangent.astype(jnp.float32).reshape(row_count, D)
    grad_four, gain_four, shift_four = norm_back(grad_final, final_normal, final_inv, gain_rows[4])
    grad_mid, grad_up_two, grad_down_two, gain_three, shift_three = feed_back(
        0.5 * grad_four, saved_four, gain_rows[3], up_two, down_two
    )
    grad_three = grad_four + grad_mid
    narrow_low = grad_three.astype(jnp.bfloat16)
    grad_narrow = product_tn(swish_low, narrow_low)
    grad_batch = (product_nt(narrow_low, narrow_full) * swish_grad(bn_flat)).reshape(
        utt_count, stretch_len, D
    )
    gain_batch = jnp.sum(grad_batch * bn_normal, axis=(0, 1))
    shift_batch = jnp.sum(grad_batch, axis=(0, 1))
    grad_hat = grad_batch * gain_rows[5]
    total_hat, total_cross = lax.psum(
        (jnp.sum(grad_hat, axis=(0, 1)), jnp.sum(grad_hat * bn_normal, axis=(0, 1))), ("dp", "tm")
    )
    grad_depth = bn_inv * (
        grad_hat - live_col / total_count * (total_hat + bn_normal * total_cross)
    )
    grad_framed = padded_2(grad_depth.astype(jnp.bfloat16), (("tm", 1),), pad_width).astype(
        grad_depth.dtype
    )
    grad_gated = kernel_taps[0] * grad_framed[:, KW - 1 : KW - 1 + stretch_len]
    for offset in range(1, KW):
        grad_gated = (
            grad_gated
            + kernel_taps[offset] * grad_framed[:, KW - 1 - offset : KW - 1 - offset + stretch_len]
        )
    grad_taps = jnp.stack(
        [
            jnp.sum(grad_depth * framed[:, offset : offset + stretch_len], axis=(0, 1))
            for offset in range(KW)
        ]
    )
    grad_glu = (grad_gated * live_col).reshape(row_count, D)
    grad_wide_out = jnp.concatenate(
        [grad_glu * gate_sig, grad_glu * lin_half * gate_sig * (1.0 - gate_sig)], axis=1
    ).astype(jnp.bfloat16)
    grad_wide = product_tn(conv_low, grad_wide_out)
    grad_conv_in, gain_two, shift_two = norm_back(
        product_nt(grad_wide_out, wide_full), conv_normal, conv_inv, gain_rows[2]
    )
    grad_two = grad_three + grad_conv_in
    merge_low = grad_two.astype(jnp.bfloat16)
    grad_merge = product_tn(attended_low, merge_low)
    grad_attended = product_nt(merge_low, merge_full).astype(jnp.bfloat16)
    grad_heads_u, grad_heads_v, grad_key_heads, grad_value_heads, grad_rel_heads = lax.map(
        head_backward,
        (heads_u, heads_v, key_store, value_store, rel_heads, log_totals, to_heads(grad_attended)),
    )
    grad_query_u = from_heads(grad_heads_u)
    grad_query_v = from_heads(grad_heads_v)
    grad_biases = jnp.stack([jnp.sum(grad_query_u, axis=0), jnp.sum(grad_query_v, axis=0)])
    grad_rel_flat = grad_rel_heads.transpose(1, 0, 2).reshape(rel_span, D)
    grad_rel_proj = lax.dot_general(
        table_low.astype(jnp.float32),
        grad_rel_flat,
        (((0,), (0,)), ((), ())),
        precision=lax.Precision.HIGHEST,
        preferred_element_type=jnp.float32,
    )
    grad_joint_out = jnp.concatenate(
        [grad_query_u + grad_query_v, from_heads(grad_key_heads), from_heads(grad_value_heads)],
        axis=1,
    ).astype(jnp.bfloat16)
    grad_joint = product_tn(att_low, grad_joint_out)
    grad_att_in, gain_one, shift_one = norm_back(
        product_nt(grad_joint_out, joint_full), att_normal, att_inv, gain_rows[1]
    )
    grad_one = grad_two + grad_att_in
    grad_first, grad_up_one, grad_down_one, gain_zero, shift_zero = feed_back(
        0.5 * grad_one, saved_one, gain_rows[0], up_one, down_one
    )
    grad_zero = grad_one + grad_first
    grad_gains = jnp.stack([gain_zero, gain_one, gain_two, gain_three, gain_four, gain_batch])
    grad_shifts = jnp.stack(
        [shift_zero, shift_one, shift_two, shift_three, shift_four, shift_batch]
    )
    summed = (
        lax.psum_scatter(
            grad_up_one.astype(jnp.bfloat16), "tm", scatter_dimension=0, tiled=True
        ).astype(jnp.float32),
        lax.psum_scatter(
            grad_down_one.astype(jnp.bfloat16), "tm", scatter_dimension=0, tiled=True
        ).astype(jnp.float32),
        lax.psum_scatter(
            grad_joint.astype(jnp.bfloat16), "tm", scatter_dimension=0, tiled=True
        ).astype(jnp.float32),
        lax.psum_scatter(
            grad_rel_proj.astype(jnp.bfloat16), "tm", scatter_dimension=0, tiled=True
        ).astype(jnp.float32),
        lax.psum_scatter(
            grad_merge.astype(jnp.bfloat16), "tm", scatter_dimension=0, tiled=True
        ).astype(jnp.float32),
        lax.psum_scatter(
            grad_wide.astype(jnp.bfloat16), "tm", scatter_dimension=0, tiled=True
        ).astype(jnp.float32),
        lax.psum_scatter(
            grad_narrow.astype(jnp.bfloat16), "tm", scatter_dimension=0, tiled=True
        ).astype(jnp.float32),
        lax.psum_scatter(
            grad_up_two.astype(jnp.bfloat16), "tm", scatter_dimension=0, tiled=True
        ).astype(jnp.float32),
        lax.psum_scatter(
            grad_down_two.astype(jnp.bfloat16), "tm", scatter_dimension=0, tiled=True
        ).astype(jnp.float32),
        lax.psum_scatter(
            grad_gains.astype(jnp.bfloat16), "tm", scatter_dimension=1, tiled=True
        ).astype(jnp.float32),
        lax.psum_scatter(
            grad_shifts.astype(jnp.bfloat16), "tm", scatter_dimension=1, tiled=True
        ).astype(jnp.float32),
        lax.psum_scatter(
            grad_biases.astype(jnp.bfloat16), "tm", scatter_dimension=1, tiled=True
        ).astype(jnp.float32),
        lax.psum_scatter(
            grad_taps.astype(jnp.bfloat16), "tm", scatter_dimension=1, tiled=True
        ).astype(jnp.float32),
    )
    summed = (
        lax.psum(summed[0].astype(jnp.bfloat16), "dp").astype(jnp.float32),
        lax.psum(summed[1].astype(jnp.bfloat16), "dp").astype(jnp.float32),
        lax.psum(summed[2].astype(jnp.bfloat16), "dp").astype(jnp.float32),
        lax.psum(summed[3].astype(jnp.bfloat16), "dp").astype(jnp.float32),
        lax.psum(summed[4].astype(jnp.bfloat16), "dp").astype(jnp.float32),
        lax.psum(summed[5].astype(jnp.bfloat16), "dp").astype(jnp.float32),
        lax.psum(summed[6].astype(jnp.bfloat16), "dp").astype(jnp.float32),
        lax.psum(summed[7].astype(jnp.bfloat16), "dp").astype(jnp.float32),
        lax.psum(summed[8].astype(jnp.bfloat16), "dp").astype(jnp.float32),
        lax.psum(summed[9].astype(jnp.bfloat16), "dp").astype(jnp.float32),
        lax.psum(summed[10].astype(jnp.bfloat16), "dp").astype(jnp.float32),
        lax.psum(summed[11].astype(jnp.bfloat16), "dp").astype(jnp.float32),
        lax.psum(summed[12].astype(jnp.bfloat16), "dp").astype(jnp.float32),
    )
    return (
        final_out.astype(jnp.bfloat16).reshape(utt_count, stretch_len, D),
        grad_zero.astype(jnp.bfloat16).reshape(utt_count, stretch_len, D),
        summed[0],
        summed[1],
        summed[2],
        summed[3],
        summed[4],
        summed[5],
        summed[6],
        summed[7],
        summed[8],
        summed[9],
        summed[10],
        summed[11],
        summed[12],
    )


def solution(mesh):
    return jax.shard_map(
        body,
        mesh=mesh,
        in_specs=(
            P("dp", "tm", None),
            P("dp", "tm", None),
            P("dp"),
            P("tm", None),
            P("tm", None),
            P("tm", None),
            P("tm", None),
            P("tm", None),
            P("tm", None),
            P("tm", None),
            P("tm", None),
            P("tm", None),
            P(None, "tm"),
            P(None, "tm"),
            P(None, "tm"),
            P(None, "tm"),
        ),
        out_specs=(
            P("dp", "tm", None),
            P("dp", "tm", None),
            P("tm", None),
            P("tm", None),
            P("tm", None),
            P("tm", None),
            P("tm", None),
            P("tm", None),
            P("tm", None),
            P("tm", None),
            P("tm", None),
            P(None, "tm"),
            P(None, "tm"),
            P(None, "tm"),
            P(None, "tm"),
        ),
        check_vma=False,
    )
```

profile of v0, /device:TPU:11, one launch (start us, length us, event | category | flops | bytes accessed | tf_op | source)
XLA Modules:
  0.0 5476.7 jit_solution(3298114813867431200)
XLA Ops:
  109.8 73.9 %all-gather.34.cloned.1.call-done = bf16[1024,4096]{1,0:T(8,128)(2,1)} async-done(((bf16[128,4096]{1,0:T(8,128)(2,1)}), bf16[1024,4096]{1,0:T(8,128)(2,1)}) %all-gather.34.cloned.1.call-update) | async-done | bytes 8388624 | tf_op jit(solution)/shard_map/all_gather | solution.py:148
  202.6 106.3 %all-gather.36.cloned.1.call-done = bf16[4096,1024]{1,0:T(8,128)(2,1)} async-done(((bf16[512,1024]{1,0:T(8,128)(2,1)}), bf16[4096,1024]{1,0:T(8,128)(2,1)}) %all-gather.36.cloned.1.call-update) | async-done | bytes 8388624 | tf_op jit(solution)/shard_map/all_gather | solution.py:149
  325.5 82.8 %all-gather.38.cloned.1.call-done = bf16[1024,3072]{1,0:T(8,128)(2,1)} async-done(((bf16[128,3072]{1,0:T(8,128)(2,1)}), bf16[1024,3072]{1,0:T(8,128)(2,1)}) %all-gather.38.cloned.1.call-update) | async-done | bytes 6291472 | tf_op jit(solution)/shard_map/all_gather | solution.py:150
  429.4 878.4 %while.36 = (s32[]{:T(128)}, bf16[8,4,256,128]{3,2,1,0:T(8,128)(2,1)}, f32[8,4,256]{2,1,0:T(4,128)}, bf16[8,4,256,128]{3,2,1,0:T(8,128)(2,1)}, bf16[8,4,256,128]...) while((s32[]{:T(128)}, ...), condition=%wide.region_7.8_spmd.clone.clone, body=%wide.region_4.7_spmd.clone.sunk.clone | while | flops 1696340992 | bytes 191935728 | solution.py:274
  1367.0 64.8 %all-gather.44.cloned.1.call-done = bf16[1024,2048]{1,0:T(8,128)(2,1)} async-done(((bf16[128,2048]{1,0:T(8,128)(2,1)}), bf16[1024,2048]{1,0:T(8,128)(2,1)}) %all-gather.44.cloned.1.call-update) | async-done | bytes 4194320 | tf_op jit(solution)/shard_map/all_gather | solution.py:153
  1625.8 108.6 %all-gather.50.cloned.1.call-done = bf16[4096,1024]{1,0:T(8,128)(2,1)} async-done(((bf16[512,1024]{1,0:T(8,128)(2,1)}), bf16[4096,1024]{1,0:T(8,128)(2,1)}) %all-gather.50.cloned.1.call-update) | async-done | bytes 8388624 | tf_op jit(solution)/shard_map/all_gather | solution.py:156
  1891.1 2150.2 %while.37 = (s32[]{:T(128)}, f32[8,4,256,128]{3,2,1,0:T(8,128)}, f32[8,4,256,128]{3,2,1,0:T(8,128)}, bf16[8,4,256,128]{3,2,1,0:T(8,128)(2,1)}, bf16[8,4,256,128]...) while((s32[]{:T(128)}, f32[8,4,256,128]{3,2,1,0:T(8,128)}, ...), condition=%wide.region_34.35_spmd.clone.clone, body=%wide.region_30.34_spmd.clone.sunk.clone | while | flops 4520451072 | bytes 350419392 | solution.py:353
  2089.4 67.3 %reduce-scatter.52.cloned.1.call-done = bf16[4,256,128]{2,1,0:T(8,128)(2,1)} async-done(((bf16[4,2048,128]{2,1,0:T(8,128)(2,1)}), bf16[4,256,128]{2,1,0:T(8,128)(2,1)}) %reduce-scatter.52.cloned.1.call-update) | async-done | bytes 262160 | tf_op jit(solution)/shard_map/while/body/eval_jaxpr/reduce_scatter | solution.py:248
  2357.8 66.9 %reduce-scatter.52.cloned.1.call-done = bf16[4,256,128]{2,1,0:T(8,128)(2,1)} async-done(((bf16[4,2048,128]{2,1,0:T(8,128)(2,1)}), bf16[4,256,128]{2,1,0:T(8,128)(2,1)}) %reduce-scatter.52.cloned.1.call-update) | async-done | bytes 262160 | tf_op jit(solution)/shard_map/while/body/eval_jaxpr/reduce_scatter | solution.py:248
  2625.9 66.8 %reduce-scatter.52.cloned.1.call-done = bf16[4,256,128]{2,1,0:T(8,128)(2,1)} async-done(((bf16[4,2048,128]{2,1,0:T(8,128)(2,1)}), bf16[4,256,128]{2,1,0:T(8,128)(2,1)}) %reduce-scatter.52.cloned.1.call-update) | async-done | bytes 262160 | tf_op jit(solution)/shard_map/while/body/eval_jaxpr/reduce_scatter | solution.py:248
  2893.9 66.9 %reduce-scatter.52.cloned.1.call-done = bf16[4,256,128]{2,1,0:T(8,128)(2,1)} async-done(((bf16[4,2048,128]{2,1,0:T(8,128)(2,1)}), bf16[4,256,128]{2,1,0:T(8,128)(2,1)}) %reduce-scatter.52.cloned.1.call-update) | async-done | bytes 262160 | tf_op jit(solution)/shard_map/while/body/eval_jaxpr/reduce_scatter | solution.py:248
  3161.6 66.7 %reduce-scatter.52.cloned.1.call-done = bf16[4,256,128]{2,1,0:T(8,128)(2,1)} async-done(((bf16[4,2048,128]{2,1,0:T(8,128)(2,1)}), bf16[4,256,128]{2,1,0:T(8,128)(2,1)}) %reduce-scatter.52.cloned.1.call-update) | async-done | bytes 262160 | tf_op jit(solution)/shard_map/while/body/eval_jaxpr/reduce_scatter | solution.py:248
  3429.2 66.5 %reduce-scatter.52.cloned.1.call-done = bf16[4,256,128]{2,1,0:T(8,128)(2,1)} async-done(((bf16[4,2048,128]{2,1,0:T(8,128)(2,1)}), bf16[4,256,128]{2,1,0:T(8,128)(2,1)}) %reduce-scatter.52.cloned.1.call-update) | async-done | bytes 262160 | tf_op jit(solution)/shard_map/while/body/eval_jaxpr/reduce_scatter | solution.py:248
  3696.6 66.9 %reduce-scatter.52.cloned.1.call-done = bf16[4,256,128]{2,1,0:T(8,128)(2,1)} async-done(((bf16[4,2048,128]{2,1,0:T(8,128)(2,1)}), bf16[4,256,128]{2,1,0:T(8,128)(2,1)}) %reduce-scatter.52.cloned.1.call-update) | async-done | bytes 262160 | tf_op jit(solution)/shard_map/while/body/eval_jaxpr/reduce_scatter | solution.py:248
  3964.8 66.7 %reduce-scatter.52.cloned.1.call-done = bf16[4,256,128]{2,1,0:T(8,128)(2,1)} async-done(((bf16[4,2048,128]{2,1,0:T(8,128)(2,1)}), bf16[4,256,128]{2,1,0:T(8,128)(2,1)}) %reduce-scatter.52.cloned.1.call-update) | async-done | bytes 262160 | tf_op jit(solution)/shard_map/while/body/eval_jaxpr/reduce_scatter | solution.py:248
  4253.6 92.7 %reduce-scatter.34.cloned.1.call-done = bf16[128,2048]{1,0:T(8,128)(2,1)} async-done(((bf16[1024,2048]{1,0:T(8,128)(2,1)}), bf16[128,2048]{1,0:T(8,128)(2,1)}) %reduce-scatter.34.cloned.1.call-update) | async-done | bytes 524304 | tf_op jit(solution)/shard_map/reduce_scatter | solution.py:401
  4346.3 120.8 %reduce-scatter.28.cloned.1.call-done = bf16[128,3072]{1,0:T(8,128)(2,1)} async-done(((bf16[1024,3072]{1,0:T(8,128)(2,1)}), bf16[128,3072]{1,0:T(8,128)(2,1)}) %reduce-scatter.28.cloned.1.call-update) | async-done | bytes 786448 | tf_op jit(solution)/shard_map/reduce_scatter | solution.py:392
  4467.1 151.5 %reduce-scatter.38.cloned.1.call-done = bf16[128,4096]{1,0:T(8,128)(2,1)} async-done(((bf16[1024,4096]{1,0:T(8,128)(2,1)}), bf16[128,4096]{1,0:T(8,128)(2,1)}) %reduce-scatter.38.cloned.1.call-update) | async-done | bytes 1048592 | tf_op jit(solution)/shard_map/reduce_scatter | solution.py:407
  4618.6 151.5 %reduce-scatter.40.cloned.1.call-done = bf16[512,1024]{1,0:T(8,128)(2,1)} async-done(((bf16[4096,1024]{1,0:T(8,128)(2,1)}), bf16[512,1024]{1,0:T(8,128)(2,1)}) %reduce-scatter.40.cloned.1.call-update) | async-done | bytes 1048592 | tf_op jit(solution)/shard_map/reduce_scatter | solution.py:410
  4770.1 152.1 %reduce-scatter.24.cloned.1.call-done = bf16[128,4096]{1,0:T(8,128)(2,1)} async-done(((bf16[1024,4096]{1,0:T(8,128)(2,1)}), bf16[128,4096]{1,0:T(8,128)(2,1)}) %reduce-scatter.24.cloned.1.call-update) | async-done | bytes 1048592 | tf_op jit(solution)/shard_map/reduce_scatter | solution.py:386
  4922.2 151.5 %reduce-scatter.26.cloned.1.call-done = bf16[512,1024]{1,0:T(8,128)(2,1)} async-done(((bf16[4096,1024]{1,0:T(8,128)(2,1)}), bf16[512,1024]{1,0:T(8,128)(2,1)}) %reduce-scatter.26.cloned.1.call-update) | async-done | bytes 1048592 | tf_op jit(solution)/shard_map/reduce_scatter | solution.py:389
  5202.6 63.8 %reduce-scatter.42.cloned.1.call-done = bf16[128,6]{1,0:T(8,128)(2,1)} async-done(((bf16[1024,6]{1,0:T(8,128)(2,1)}), bf16[128,6]{1,0:T(8,128)(2,1)}) %reduce-scatter.42.cloned.1.call-update) | async-done | bytes 1552
  5267.3 63.9 %reduce-scatter.44.cloned.1.call-done = bf16[128,6]{1,0:T(8,128)(2,1)} async-done(((bf16[1024,6]{1,0:T(8,128)(2,1)}), bf16[128,6]{1,0:T(8,128)(2,1)}) %reduce-scatter.44.cloned.1.call-update) | async-done | bytes 1552
  5342.0 114.2 %all-reduce.8.cloned.1.call-done = (bf16[128,4096]{1,0:T(8,128)(2,1)}, bf16[512,1024]{1,0:T(8,128)(2,1)}, bf16[128,3072]{1,0:T(8,128)(2,1)}, bf16[128,1024]{1,0:...) async-done(((bf16[128,4096]{1,0:T(8,128)(2,1)}, ...) | async-done | bytes 6291472 | tf_op jit(solution)/shard_map/psum | solution.py:427
  (1025 shorter events, 3406.6 us)
Async XLA Ops:
  8.7 300.3 %all-gather.36.cloned.1.call-start = ((), (), s32[]{:S(2)}) async-start(), calls=%async_computation.16 | async-start | bytes 9437184 | tf_op jit(solution)/shard_map/all_gather | solution.py:149
  9.4 398.9 %all-gather.38.cloned.1.call-start = ((), (), s32[]{:S(2)}) async-start(), calls=%async_computation.17 | async-start | bytes 7077888 | tf_op jit(solution)/shard_map/all_gather | solution.py:150
  1309.3 245.7 %all-gather.46.cloned.1.call-start = ((), (), s32[]{:S(2)}) async-start(), calls=%async_computation.21 | async-start | bytes 2359296 | tf_op jit(solution)/shard_map/all_gather | solution.py:154
  1310.0 299.1 %all-gather.48.cloned.1.call-start = ((), (), s32[]{:S(2)}) async-start(), calls=%async_computation.22 | async-start | bytes 9437184 | tf_op jit(solution)/shard_map/all_gather | solution.py:155
  1310.6 423.8 %all-gather.50.cloned.1.call-start = ((), (), s32[]{:S(2)}) async-start(), calls=%async_computation.23 | async-start | bytes 9437184 | tf_op jit(solution)/shard_map/all_gather | solution.py:156
  2162.3 193.8 %reduce-scatter.50.cloned.1.call-start = ((), (), s32[]{:S(2)}) async-start(), calls=%async_computation.42 | async-start | bytes 2359296 | tf_op jit(solution)/shard_map/while/body/eval_jaxpr/reduce_scatter | solution.py:245
  2430.3 193.9 %reduce-scatter.50.cloned.1.call-start = ((), (), s32[]{:S(2)}) async-start(), calls=%async_computation.42 | async-start | bytes 2359296 | tf_op jit(solution)/shard_map/while/body/eval_jaxpr/reduce_scatter | solution.py:245
  2698.3 193.9 %reduce-scatter.50.cloned.1.call-start = ((), (), s32[]{:S(2)}) async-start(), calls=%async_computation.42 | async-start | bytes 2359296 | tf_op jit(solution)/shard_map/while/body/eval_jaxpr/reduce_scatter | solution.py:245
  2966.3 193.6 %reduce-scatter.50.cloned.1.call-start = ((), (), s32[]{:S(2)}) async-start(), calls=%async_computation.42 | async-start | bytes 2359296 | tf_op jit(solution)/shard_map/while/body/eval_jaxpr/reduce_scatter | solution.py:245
  3501.2 193.8 %reduce-scatter.50.cloned.1.call-start = ((), (), s32[]{:S(2)}) async-start(), calls=%async_computation.42 | async-start | bytes 2359296 | tf_op jit(solution)/shard_map/while/body/eval_jaxpr/reduce_scatter | solution.py:245
  3769.2 193.9 %reduce-scatter.50.cloned.1.call-start = ((), (), s32[]{:S(2)}) async-start(), calls=%async_computation.42 | async-start | bytes 2359296 | tf_op jit(solution)/shard_map/while/body/eval_jaxpr/reduce_scatter | solution.py:245
  4041.3 194.5 %reduce-scatter.36.cloned.1.call-start = ((), (), s32[]{:S(2)}) async-start(), calls=%async_computation.30 | async-start | bytes 2359296 | tf_op jit(solution)/shard_map/reduce_scatter | solution.py:404
  4041.9 193.9 %reduce-scatter.30.cloned.1.call-start = ((), (), s32[]{:S(2)}) async-start(), calls=%async_computation.27 | async-start | bytes 2359296 | tf_op jit(solution)/shard_map/reduce_scatter | solution.py:395
  4070.9 275.4 %reduce-scatter.34.cloned.1.call-start = ((), (), s32[]{:S(2)}) async-start(), calls=%async_computation.29 | async-start | bytes 4718592 | tf_op jit(solution)/shard_map/reduce_scatter | solution.py:401
  4092.0 375.1 %reduce-scatter.28.cloned.1.call-start = ((), (), s32[]{:S(2)}) async-start(), calls=%async_computation.26 | async-start | bytes 7077888 | tf_op jit(solution)/shard_map/reduce_scatter | solution.py:392
  4115.1 503.5 %reduce-scatter.38.cloned.1.call-start = ((), (), s32[]{:S(2)}) async-start(), calls=%async_computation.31 | async-start | bytes 9437184 | tf_op jit(solution)/shard_map/reduce_scatter | solution.py:407
  4131.3 638.8 %reduce-scatter.40.cloned.1.call-start = ((), (), s32[]{:S(2)}) async-start(), calls=%async_computation.32 | async-start | bytes 9437184 | tf_op jit(solution)/shard_map/reduce_scatter | solution.py:410
  4147.7 774.5 %reduce-scatter.24.cloned.1.call-start = ((), (), s32[]{:S(2)}) async-start(), calls=%async_computation.24 | async-start | bytes 9437184 | tf_op jit(solution)/shard_map/reduce_scatter | solution.py:386
  4198.2 875.5 %reduce-scatter.26.cloned.1.call-start = ((), (), s32[]{:S(2)}) async-start(), calls=%async_computation.25 | async-start | bytes 9437184 | tf_op jit(solution)/shard_map/reduce_scatter | solution.py:389
  4213.7 923.9 %reduce-scatter.48.cloned.1.call-start = ((), (), s32[]{:S(2)}) async-start(), calls=%async_computation.36 | async-start | bytes 294912
  4215.4 986.4 %reduce-scatter.46.cloned.1.call-start = ((), (), s32[]{:S(2)}) async-start(), calls=%async_computation.35 | async-start | bytes 294912
  4216.5 1050.0 %reduce-scatter.42.cloned.1.call-start = ((), (), s32[]{:S(2)}) async-start(), calls=%async_computation.33 | async-start | bytes 294912
  4234.3 1096.9 %reduce-scatter.44.cloned.1.call-start = ((), (), s32[]{:S(2)}) async-start(), calls=%async_computation.34 | async-start | bytes 294912
  4235.8 1220.4 %all-reduce.8.cloned.1.call-start = ((), (), s32[]{:S(2)}) async-start(), calls=%async_computation.37 | async-start | bytes 12582912 | tf_op jit(solution)/shard_map/psum | solution.py:427
  (215 other events, 12437.8 us)
Sparse Core Ops, SparseCore 0:
  61.2 122.4 all-gather.33
  185.8 123.1 all-gather.35
  311.0 97.2 all-gather.37
  1360.7 71.0 all-gather.43
  1485.5 123.5 all-gather.47
  1611.2 123.1 all-gather.49
  2089.4 67.3 reduce-scatter.51
  2357.4 67.3 reduce-scatter.51
  2625.6 67.0 reduce-scatter.51
  2893.5 67.2 reduce-scatter.51
  3161.3 67.0 reduce-scatter.51
  3428.6 67.0 reduce-scatter.51
  3696.2 67.2 reduce-scatter.51
  3964.4 67.0 reduce-scatter.51
  4045.4 66.6 reduce-scatter.35
  4116.0 66.7 reduce-scatter.29
  4186.9 66.6 reduce-scatter.31
  4257.2 88.9 reduce-scatter.33
  4350.3 116.7 reduce-scatter.27
  4471.0 147.5 reduce-scatter.37
  4622.0 147.9 reduce-scatter.39
  4774.1 147.9 reduce-scatter.23
  4925.7 147.9 reduce-scatter.25
  5334.4 121.7 all-reduce.7
  (47 shorter events, 2450.1 us)
where the time goes:
time: 5490 us; the launch traced here: 5480 us
  waiting for transfers between devices  2550 us (46%)
  local copies, waits for them, and re-layouts  1610 us (29%)
  matrix products  847 us (15%)
  blocking collectives  207 us (4%)
  other arithmetic  200 us (4%)
    while x144, local copies, waits for them, and re-layouts  567 us
    reduce_scatter x8, waiting for transfers between devices, head_backward(): lax.psum_scatter(grad_values.astype(jnp.bfloat16), 'tm', scatter_dimensio...  535 us
    reshape x16, local copies, waits for them, and re-layouts, rel_shift(): flattened.reshape(lead_dims + (row_count, col_span - 1))[..., :key_count]  280 us
    unnamed x27, waiting for transfers between devices  256 us
    reshape x16, local copies, waits for them, and re-layouts, rel_shift(): flattened = raw.reshape(lead_dims + (row_count * col_span,))  188 us
    slice x16, local copies, waits for them, and re-layouts, rel_shift(): flattened[..., row_count - 1:row_count - 1 + row_count * (col_span - 1)]  182 us
    all_gather x8, waiting for transfers between devices, head_backward(): lax.all_gather(key_src, 'tm', axis=1, tiled=True)  161 us
    reduce_scatter x1, waiting for transfers between devices, body(): lax.psum_scatter(grad_up_one.astype(jnp.bfloat16), 'tm', scatter_dimensio...  152 us
  transfers between devices with their start and end apart: 75, of which 43 were waited for; matrix products, arithmetic and copies ran while one was open for 40% of the time, Pallas kernels for 0%

commit v1 on v0

v1 whole, which is shorter than its diff:
```python
import functools
import math

import jax
import jax.numpy as jnp
from jax import lax
from jax.experimental import pallas as pl
from jax.experimental.pallas import tpu as pltpu
from jax.sharding import PartitionSpec as P

D = 1024
HEADS = 8
HEAD_DIM = 128
KW = 5

AXES = ("dp", "tm")
LOG2E = math.log2(math.e)
eps_norm = 1e-05
neg_fill = -1e30
f32 = jnp.float32
bf16 = jnp.bfloat16


def product(left, right):
    return jnp.dot(left, right, preferred_element_type=f32)


def product_nt(left, right):
    return lax.dot_general(left, right, (((1,), (1,)), ((), ())), preferred_element_type=f32)


def product_tn(left, right):
    return lax.dot_general(left, right, (((0,), (0,)), ((), ())), preferred_element_type=f32)


def tile_start(own, tile_at, rows, tile):
    per = rows // tile
    return ((tile_at // per) ^ own) * rows + (tile_at % per) * tile


def biased_queries(q_ref, bias_ref):
    query = q_ref[0].astype(f32)
    scale = HEAD_DIM**-0.5 * LOG2E
    query_u = ((query + bias_ref[0:1, :]) * scale).astype(bf16)
    query_v = ((query + bias_ref[1:2, :]) * scale).astype(bf16)
    return query_u, query_v


def slot_scores(query_u, query_v, key, rel_window, mask_row, rows, tile):
    width = rows + tile
    raw = product_nt(query_v, rel_window)
    shifted = pltpu.roll(raw, width - (tile - 1), 1, stride=1, stride_axis=0)[:, :rows]
    return shifted + product_nt(query_u, key) + mask_row


def attend_kernel(
    own_ref, q_ref, k_ref, v_ref, rel_ref, bias_ref, mask_ref, out_ref, lse_ref, score_ref,
    *, slots, rows, tile
):
    own = own_ref[0]
    start = tile_start(own, pl.program_id(1), rows, tile)
    query_u, query_v = biased_queries(q_ref, bias_ref)
    top = jnp.full((tile, 1), -jnp.inf, f32)
    for s in range(slots):
        base = pl.multiple_of(slots * rows - tile - start + (own ^ s) * rows, tile)
        scores = slot_scores(
            query_u, query_v, k_ref[s], rel_ref[pl.ds(base, rows + tile), :],
            mask_ref[0:1, s * rows : (s + 1) * rows], rows, tile,
        )
        score_ref[s] = scores
        top = jnp.maximum(top, jnp.max(scores, axis=1, keepdims=True))
    total = jnp.zeros((tile, 1), f32)
    mixed = jnp.zeros((tile, HEAD_DIM), f32)
    for s in range(slots):
        weights = jnp.exp2(score_ref[s] - top)
        total = total + jnp.sum(weights, axis=1, keepdims=True)
        mixed = mixed + product(weights.astype(bf16), v_ref[s])
    out_ref[0] = (mixed / total).astype(bf16)
    lse_ref[0] = top + jnp.log2(total)


def attend_back_kernel(
    own_ref, q_ref, k_ref, v_ref, rel_ref, bias_ref, mask_ref, o_ref, do_ref, lse_ref,
    dq_ref, dk_ref, dv_ref, drel_ref, dbias_ref, dk_acc, dv_acc, *, slots, rows, tile
):
    own = own_ref[0]
    tile_at = pl.program_id(1)
    start = tile_start(own, tile_at, rows, tile)
    scale = HEAD_DIM**-0.5

    @pl.when(tile_at == 0)
    def _():
        dk_acc[...] = jnp.zeros_like(dk_acc)
        dv_acc[...] = jnp.zeros_like(dv_acc)
        drel_ref[...] = jnp.zeros_like(drel_ref)
        dbias_ref[...] = jnp.zeros_like(dbias_ref)

    query_u, query_v = biased_queries(q_ref, bias_ref)
    grad_out = do_ref[0]
    inner = jnp.sum(grad_out.astype(f32) * o_ref[0].astype(f32), axis=1, keepdims=True)
    lse = lse_ref[0]
    width = rows + tile
    row_at = lax.broadcasted_iota(jnp.int32, (tile, tile), 0)
    col_at = lax.broadcasted_iota(jnp.int32, (tile, tile), 1)
    flip = (row_at + col_at == tile - 1).astype(bf16)
    query_v_flip = product(flip, query_v).astype(bf16)
    grad_u = jnp.zeros((tile, HEAD_DIM), f32)
    grad_v_flip = jnp.zeros((tile, HEAD_DIM), f32)
    for s in range(slots):
        base = pl.multiple_of(slots * rows - tile - start + (own ^ s) * rows, tile)
        rel_window = rel_ref[pl.ds(base, width), :]
        key = k_ref[s]
        scores = slot_scores(
            query_u, query_v, key, rel_window, mask_ref[0:1, s * rows : (s + 1) * rows], rows, tile
        )
        probs = jnp.exp2(scores - lse)
        grad_probs = product_nt(grad_out, v_ref[s])
        grad_scores = (probs * (grad_probs - inner)).astype(bf16)
        dv_acc[s] += product_tn(probs.astype(bf16), grad_out)
        dk_acc[s] += product_tn(grad_scores, query_u)
        grad_u = grad_u + product(grad_scores, key)
        flipped = product(flip, grad_scores).astype(bf16)
        padded = jnp.concatenate([flipped, jnp.zeros((tile, width - rows), bf16)], axis=1)
        grad_raw = pltpu.roll(padded, 0, 1, stride=1, stride_axis=0)
        grad_v_flip = grad_v_flip + product(grad_raw, rel_window)
        drel_ref[pl.ds(base, width), :] += product_tn(grad_raw, query_v_flip)
    high = grad_v_flip.astype(bf16)
    low = (grad_v_flip - high.astype(f32)).astype(bf16)
    grad_v = product(flip, high) + product(flip, low)
    dbias_ref[0, 0:1, :] += jnp.sum(grad_u, axis=0, keepdims=True) * scale
    dbias_ref[0, 1:2, :] += jnp.sum(grad_v, axis=0, keepdims=True) * scale
    dq_ref[0] = ((grad_u + grad_v) * scale).astype(bf16)

    @pl.when(tile_at == pl.num_programs(1) - 1)
    def _():
        dk_ref[...] = (dk_acc[...] * (1.0 / LOG2E)).astype(bf16)
        dv_ref[...] = dv_acc[...].astype(bf16)
        drel_ref[...] = drel_ref[...] * (1.0 / LOG2E)


def attention_specs(slots, rows, heads, tile):
    per = rows // tile
    span = slots * rows
    by_tile = pl.BlockSpec((1, tile, HEAD_DIM), lambda h, i, own: (i // per, i % per, h))
    in_specs = [
        by_tile,
        pl.BlockSpec((slots, rows, HEAD_DIM), lambda h, i, own: (0, 0, heads + h)),
        pl.BlockSpec((slots, rows, HEAD_DIM), lambda h, i, own: (0, 0, 2 * heads + h)),
        pl.BlockSpec((2 * span, HEAD_DIM), lambda h, i, own: (0, h)),
        pl.BlockSpec((2, HEAD_DIM), lambda h, i, own: (0, h)),
        pl.BlockSpec((1, span), lambda h, i, own: (0, 0)),
    ]
    return (heads, slots * per), by_tile, in_specs


def attend(own, joint, rel, bias, mask):
    slots, rows, wide = joint.shape
    heads = wide // (3 * HEAD_DIM)
    span, tile = slots * rows, min(256, rows)
    grid, by_tile, in_specs = attention_specs(slots, rows, heads, tile)
    return pl.pallas_call(
        functools.partial(attend_kernel, slots=slots, rows=rows, tile=tile),
        grid_spec=pltpu.PrefetchScalarGridSpec(
            num_scalar_prefetch=1,
            grid=grid,
            in_specs=in_specs,
            out_specs=[by_tile, pl.BlockSpec((1, tile, 1), lambda h, i, own: (h, i, 0))],
            scratch_shapes=[pltpu.VMEM((slots, tile, rows), f32)],
        ),
        out_shape=[
            jax.ShapeDtypeStruct((slots, rows, heads * HEAD_DIM), bf16),
            jax.ShapeDtypeStruct((heads, span, 1), f32),
        ],
        compiler_params=pltpu.CompilerParams(vmem_limit_bytes=56 << 20),
        cost_estimate=pl.CostEstimate(
            flops=heads * span * span * HEAD_DIM * 8,
            bytes_accessed=heads * span * HEAD_DIM * 20,
            transcendentals=heads * span * span,
        ),
        name="attend",
    )(own, joint, joint, joint, rel, bias, mask)


def attend_back(own, joint, rel, bias, mask, out, grad_out, lse):
    slots, rows, wide = joint.shape
    heads = wide // (3 * HEAD_DIM)
    span, tile = slots * rows, min(256, rows)
    grid, by_tile, in_specs = attention_specs(slots, rows, heads, tile)
    by_head = pl.BlockSpec((slots, rows, HEAD_DIM), lambda h, i, own: (0, 0, h))
    return pl.pallas_call(
        functools.partial(attend_back_kernel, slots=slots, rows=rows, tile=tile),
        grid_spec=pltpu.PrefetchScalarGridSpec(
            num_scalar_prefetch=1,
            grid=grid,
            in_specs=in_specs
            + [by_tile, by_tile, pl.BlockSpec((1, tile, 1), lambda h, i, own: (h, i, 0))],
            out_specs=[
                by_tile,
                by_head,
                by_head,
                pl.BlockSpec((2 * span, HEAD_DIM), lambda h, i, own: (0, h)),
                pl.BlockSpec((1, 2, HEAD_DIM), lambda h, i, own: (h, 0, 0)),
            ],
            scratch_shapes=[pltpu.VMEM((slots, rows, HEAD_DIM), f32)] * 2,
        ),
        out_shape=[jax.ShapeDtypeStruct((slots, rows, heads * HEAD_DIM), bf16)] * 3
        + [
            jax.ShapeDtypeStruct((2 * span, heads * HEAD_DIM), f32),
            jax.ShapeDtypeStruct((heads, 2, HEAD_DIM), f32),
        ],
        compiler_params=pltpu.CompilerParams(vmem_limit_bytes=56 << 20),
        cost_estimate=pl.CostEstimate(
            flops=heads * span * span * HEAD_DIM * 22,
            bytes_accessed=heads * span * HEAD_DIM * 40,
            transcendentals=heads * span * span,
        ),
        name="attend_back",
    )(own, joint, joint, joint, rel, bias, mask, out, grad_out, lse)


def norm_fwd(values, gain_row, shift_row):
    centered = values - jnp.mean(values, axis=-1, keepdims=True)
    scale_inv = lax.rsqrt(jnp.mean(centered * centered, axis=-1, keepdims=True) + eps_norm)
    normal = centered * scale_inv
    return (normal * gain_row + shift_row, normal, scale_inv)


def norm_back(grad_out, normal, scale_inv, gain_row):
    grad_norm = grad_out * gain_row
    grad_in = scale_inv * (
        grad_norm
        - jnp.mean(grad_norm, axis=-1, keepdims=True)
        - normal * jnp.mean(grad_norm * normal, axis=-1, keepdims=True)
    )
    return (grad_in, jnp.sum(grad_out * normal, axis=0), jnp.sum(grad_out, axis=0))


def swish_grad(values):
    sigmoid_val = jax.nn.sigmoid(values)
    return sigmoid_val * (1.0 + values * (1.0 - sigmoid_val))


def sinusoid(distance, feat_width):
    half_width = feat_width // 2
    inv_freq = jnp.exp(jnp.arange(half_width, dtype=f32) * (-2.0 * math.log(10000.0) / feat_width))
    angles = distance[:, None] * inv_freq[None, :]
    return jnp.concatenate([jnp.sin(angles), jnp.cos(angles)], axis=1)


class Layout:
    def __init__(self, utt_count):
        self.dp, self.tm, self.utt = lax.axis_size("dp"), lax.axis_size("tm"), utt_count
        self.pairs = self.dp // 2
        self.size = self.tm // utt_count
        self.subs = self.size // 2
        dp_at, t = lax.axis_index("dp"), lax.axis_index("tm")
        self.core, self.t = dp_at % 2, t
        group, self.sub = t // self.subs, t % self.subs
        self.home_core, self.home_slot = group % 2, group // 2
        self.own = self.core * self.subs + self.sub

    def route(self, target):
        pairs = []
        for p in range(self.pairs):
            for c in range(2):
                for t in range(self.tm):
                    tp, tc, tt = target(p, c, t)
                    pairs.append(((2 * p + c) * self.tm + t, (2 * tp + tc) * self.tm + tt))
        return pairs

    def send(self, values, target):
        return lax.ppermute(values, AXES, self.route(target))

    def to_class(self, step):
        def target(p, c, t):
            other = (c * self.subs + t % self.subs) ^ step
            return p, other // self.subs, t - t % self.subs + other % self.subs

        return target

    def to_core(self, p, c, t):
        return p, 1 - c, t

    def home(self, step):
        def target(p, c, t):
            kind, at = t // self.utt, t % self.utt
            place = (step + at) % self.utt
            return p, kind // self.subs, (2 * place + c) * self.subs + kind % self.subs

        return target

    def enter(self, shard):
        at = self.t % self.utt
        result = jnp.zeros_like(shard)
        for k in range(self.utt):
            block = lax.dynamic_index_in_dim(shard, (k + at) % self.utt, 0, keepdims=True)
            block = self.send(block, self.home(k))
            result = lax.dynamic_update_slice_in_dim(
                result, block, (self.home_slot - k) % self.utt, axis=0
            )
        return result

    def leave(self, blocks):
        at = self.t % self.utt
        result = jnp.zeros_like(blocks)
        for k in range(self.utt):
            block = lax.dynamic_index_in_dim(
                blocks, (self.home_slot - k) % self.utt, 0, keepdims=True
            )
            there = self.route(self.home(k))
            block = lax.ppermute(block, AXES, [(b, a) for a, b in there])
            result = lax.dynamic_update_slice_in_dim(result, block, (k + at) % self.utt, axis=0)
        return result

    def all_slots(self, values):
        parts = [values] + [self.send(values, self.to_class(s)) for s in range(1, self.size)]
        return jnp.concatenate(parts, axis=0)

    def own_sum(self, partial):
        parts = partial.reshape((self.size, -1) + partial.shape[1:])
        total = parts[0]
        for s in range(1, self.size):
            total = total + self.send(parts[s].astype(bf16), self.to_class(s)).astype(f32)
        return total

    def over_utterances(self, values, join):
        step = 1
        groups = 2 * self.utt
        while step < self.pairs * groups:

            def target(p, c, t, step=step):
                other = (p * groups + t // self.subs) ^ step
                return other // groups, c, (other % groups) * self.subs + t % self.subs

            values = join(values, self.send(values, target))
            step *= 2
        return values

    def core_half(self, values, axis):
        shape = values.shape
        split = values.reshape(shape[:axis] + (2, shape[axis] // 2) + shape[axis + 1 :])
        return lax.dynamic_index_in_dim(split, self.core, axis, keepdims=False)

    def sub_part(self, values, axis):
        if self.subs == 1:
            return values
        width = values.shape[axis] // self.subs
        return lax.dynamic_slice_in_dim(values, self.sub * width, width, axis)

    def sub_place(self, values, axis):
        if self.subs == 1:
            return values
        width = values.shape[axis]
        shape = list(values.shape)
        shape[axis] = width * self.subs
        return lax.dynamic_update_slice_in_dim(
            jnp.zeros(shape, values.dtype), values, self.sub * width, axis
        )

    def cols_half(self, local, groups):
        rows, cols = local.shape
        split = local.reshape(rows, groups, 2, cols // (2 * groups))
        return lax.dynamic_index_in_dim(split, self.core, 2, keepdims=False).reshape(rows, cols // 2)

    def cols_join(self, halves, groups):
        _, rows, cols = halves.shape
        split = halves.reshape(2, rows, groups, cols // groups)
        return split.transpose(1, 2, 0, 3).reshape(rows, 2 * cols)

    def gather_small(self, local):
        parts = local[None]
        step = 1
        while step < self.tm:
            parts = jnp.concatenate(
                [parts, self.send(parts, lambda p, c, t, step=step: (p, c, t ^ step))], axis=0
            )
            step *= 2
        parts = jnp.take(parts, jnp.arange(self.tm, dtype=jnp.int32) ^ self.t, axis=0)
        return parts.transpose(1, 0, 2).reshape(local.shape[0], -1)

    def sum_all(self, values):
        step = 1
        while step < self.size:
            values = values + self.send(values, self.to_class(step))
            step *= 2
        return self.over_utterances(values, jnp.add)

    def gather(self, locals_):
        plane = lax.axis_index("dp") // 2
        parts = [lax.dynamic_slice_in_dim(v, plane * (v.shape[0] // self.pairs), v.shape[0] // self.pairs, 0) for v in locals_]
        packed, places = pack(parts)
        groups = [
            [(2 * p + c) * self.tm + t for t in range(self.tm) for p in range(self.pairs)]
            for c in range(2)
        ]
        full = lax.all_gather(packed[None], AXES, axis=0, tiled=True, axis_index_groups=groups)
        return [v.reshape(-1, v.shape[-1]) for v in unpack(full, places)]

    def scatter(self, grads, over_planes=False, after=None):
        plane = lax.axis_index("dp") // 2
        split = [g.astype(bf16).reshape(self.tm, self.pairs, -1, g.shape[-1]) for g in grads]

        def part(at):
            return pack([lax.dynamic_index_in_dim(v, at, 1, keepdims=False) for v in split])

        mine, places = part(plane)
        if over_planes:
            for s in range(1, self.pairs):
                other = self.send(part(plane ^ s)[0], lambda p, c, t, s=s: (p ^ s, c, t))
                mine = (mine.astype(f32) + other.astype(f32)).astype(bf16)
        else:
            mine = jnp.stack([part(plane ^ s)[0] for s in range(self.pairs)], axis=1)
        if after is not None:
            mine, _ = lax.optimization_barrier((mine, after))
        return lax.psum_scatter(mine, "tm", scatter_dimension=0, tiled=True), places

    def collect(self, mine, places):
        plane = lax.axis_index("dp") // 2
        if mine.ndim == 4:
            parts = mine
            mine = parts[:, 0].astype(f32)
            for s in range(1, self.pairs):
                mine = mine + self.send(parts[:, s], lambda p, c, t, s=s: (p ^ s, c, t)).astype(f32)
            mine = mine.astype(bf16)
        whole = jnp.zeros((self.pairs,) + mine.shape[1:], bf16)
        whole = lax.dynamic_update_slice_in_dim(whole, mine, plane, 0)
        for s in range(1, self.pairs):
            other = self.send(mine, lambda p, c, t, s=s: (p ^ s, c, t))
            whole = lax.dynamic_update_slice_in_dim(whole, other, plane ^ s, 0)
        there = self.send(whole, self.to_core)
        both = jnp.stack(
            [jnp.where(self.core == 0, whole, there), jnp.where(self.core == 0, there, whole)]
        )
        return [v.astype(f32).reshape(2, -1, v.shape[-1]) for v in unpack(both, places)]


def pack(parts):
    blocks, places, row, spare = [], [], 0, None
    for v in parts:
        rows, cols, own = v.shape[-2], v.shape[-1], []
        for at in range(0, cols - D + 1, D):
            blocks.append([v[..., at : at + D]])
            own.append((row, 0, rows, D))
            row += rows
        if cols % D:
            piece = v[..., cols - cols % D :]
            if spare is not None and spare[1] == rows and spare[2] + cols % D <= D:
                blocks[spare[0]].append(piece)
                own.append((spare[3], spare[2], rows, cols % D))
                spare = None
            else:
                spare = (len(blocks), rows, cols % D, row)
                blocks.append([piece])
                own.append((row, 0, rows, cols % D))
                row += rows
        places.append(own)
    filled = []
    for block in blocks:
        joined = block[0] if len(block) == 1 else jnp.concatenate(block, axis=-1)
        if joined.shape[-1] < D:
            pads = [(0, 0)] * (joined.ndim - 1) + [(0, D - joined.shape[-1])]
            joined = jnp.pad(joined, pads)
        filled.append(joined)
    return jnp.concatenate(filled, axis=-2), places


def unpack(packed, places):
    results = []
    for own in places:
        pieces = [packed[..., r : r + n, c : c + m] for r, c, n, m in own]
        results.append(pieces[0] if len(pieces) == 1 else jnp.concatenate(pieces, axis=-1))
    return results


def merge_moments(left, right):
    count_a, mean_a, square_a = left[0], left[1], left[2]
    count_b, mean_b, square_b = right[0], right[1], right[2]
    count = count_a + count_b
    gap = mean_a - mean_b
    mean = (count_a * mean_a + count_b * mean_b) / count
    square = (square_a + square_b) + gap * gap * (count_a * count_b / count)
    return jnp.stack([count, mean, square])


def body(
    inputs,
    cotangent,
    lengths,
    first_up,
    first_down,
    joint_proj,
    rel_proj,
    merge_proj,
    conv_wide,
    conv_narrow,
    second_up,
    second_down,
    norm_gains,
    norm_shifts,
    pos_biases,
    depth_taps,
):
    lay = Layout(inputs.shape[0])
    utt_count, block_len, _ = inputs.shape
    tm, size, own = lay.tm, lay.size, lay.own
    rows = utt_count * block_len
    span = rows * size
    feats = D // size
    pad_width = KW // 2

    small = jnp.concatenate([norm_gains, norm_shifts, pos_biases, depth_taps], axis=0)
    small = lay.gather_small(small).astype(f32)
    gain_rows, shift_rows = small[0:6], small[6:12]

    def own_feats(values):
        count = values.shape[0]
        split = values.reshape(count, tm, 2, D // (2 * tm))
        half = lax.dynamic_index_in_dim(split, lay.core, 2, keepdims=False)
        return lay.sub_part(half.reshape(count, D // 2), 1)

    def place_feats(values):
        count = values.shape[0]
        half = lay.sub_place(values, 1).reshape(count, tm, 1, D // (2 * tm))
        pick = (jnp.arange(2) == lay.core).astype(f32)[None, None, :, None]
        return (half * pick).reshape(count, D)

    def place_heads(values):
        return lax.dynamic_update_slice_in_dim(
            jnp.zeros((values.shape[0], D), f32), values, own * feats, axis=1
        )

    bias_rows = lax.dynamic_slice_in_dim(small[12:14], own * feats, feats, axis=1)
    kernel_taps = own_feats(small[14 : 14 + KW])
    batch_gain, batch_shift = own_feats(gain_rows[5:6])[0], own_feats(shift_rows[5:6])[0]

    up_one, down_one = lay.gather([lay.cols_half(first_up, tm), lay.core_half(first_down, 0)])
    joint_half, rel_half = lay.gather([lay.cols_half(joint_proj, 3), lay.cols_half(rel_proj, 1)])
    merge_full, wide_half, narrow_half = lay.gather(
        [merge_proj, lay.cols_half(conv_wide, 2 * tm), lay.core_half(conv_narrow, 0)]
    )
    up_two, down_two = lay.gather([lay.cols_half(second_up, tm), lay.core_half(second_down, 0)])
    up_one, down_one = lay.sub_part(up_one, 1), lay.sub_part(down_one, 0)
    up_two, down_two = lay.sub_part(up_two, 1), lay.sub_part(down_two, 0)
    joint_own = lay.sub_part(joint_half.reshape(D, 3, D // 2), 2).reshape(D, 3 * feats)
    rel_own = lay.sub_part(rel_half, 1)
    wide_own = lay.sub_part(wide_half.reshape(D, 2, D // 2), 2).reshape(D, 2 * feats)
    narrow_own = lay.sub_part(narrow_half, 0)
    merge_slots = jnp.concatenate(
        [
            lax.dynamic_slice_in_dim(merge_full, (own ^ s) * feats, feats, axis=0)
            for s in range(size)
        ],
        axis=0,
    )

    def feed_forward(values, gain_row, shift_row, up_weight, down_weight):
        normed, normal, scale_inv = norm_fwd(values, gain_row, shift_row)
        normed_low = lay.all_slots(normed.astype(bf16))
        hidden = product(normed_low, up_weight)
        active_low = (hidden * jax.nn.sigmoid(hidden)).astype(bf16)
        result = lay.own_sum(product(active_low, down_weight))
        return (result, (normal, scale_inv, normed_low, hidden, active_low))

    def feed_back(grad_result, saved_acts, gain_row, up_weight, down_weight, between):
        normal, scale_inv, normed_low, hidden, active_low = saved_acts
        grad_low = lay.all_slots(grad_result.astype(bf16))
        grad_down = product_tn(active_low, grad_low).astype(bf16)
        grad_down, grad_low = lax.optimization_barrier((grad_down, grad_low))
        grad_hidden = (product_nt(grad_low, down_weight) * swish_grad(hidden)).astype(bf16)
        grad_up = product_tn(normed_low, grad_hidden).astype(bf16)
        grad_down, grad_up = lay.sub_place(grad_down, 0), lay.sub_place(grad_up, 1)
        grad_hidden, moved = between(grad_down, grad_up, grad_hidden)
        grad_values, grad_gain, grad_shift = norm_back(
            lay.own_sum(product_nt(grad_hidden, up_weight)), normal, scale_inv, gain_row
        )
        return (grad_values, moved, grad_gain, grad_shift)

    group_lengths = jnp.where(
        lay.home_core == lay.core, lengths, lay.send(lengths, lay.to_core)
    )
    length = lax.dynamic_index_in_dim(group_lengths, lay.home_slot, 0, keepdims=False)
    slot_class = jnp.arange(size, dtype=jnp.int32) ^ own
    frame_pos = slot_class[:, None] * rows + jnp.arange(rows, dtype=jnp.int32)[None, :]
    live = frame_pos < length
    live_col = live.astype(f32)[:, :, None]
    key_mask = jnp.where(live, 0.0, neg_fill).astype(f32).reshape(1, span)
    own_at = own.reshape(1).astype(jnp.int32)

    def framed_rows(values):
        last, leading = values[:, rows - pad_width :], values[:, :pad_width]
        before, after = [], []
        for s in range(size):
            kind = own ^ s
            prev = lax.dynamic_index_in_dim(last, jnp.maximum(kind - 1, 0) ^ own, 0)
            following = lax.dynamic_index_in_dim(
                leading, jnp.minimum(kind + 1, size - 1) ^ own, 0
            )
            before.append(jnp.where(kind > 0, prev, 0.0))
            after.append(jnp.where(kind < size - 1, following, 0.0))
        return jnp.concatenate(
            [jnp.concatenate(before, axis=0), values, jnp.concatenate(after, axis=0)], axis=1
        )

    distance = (span - 1 - jnp.arange(2 * span, dtype=jnp.int32)).astype(f32)
    table_low = sinusoid(distance, D).astype(bf16)
    up_one, table_low = lax.optimization_barrier((up_one, table_low))
    section_zero = lay.enter(inputs).astype(f32).reshape(rows, D)
    branch_one, saved_one = feed_forward(
        section_zero, gain_rows[0], shift_rows[0], up_one, down_one
    )
    section_one = section_zero + 0.5 * branch_one
    att_normed, att_normal, att_inv = norm_fwd(section_one, gain_rows[1], shift_rows[1])
    att_low = lay.all_slots(att_normed.astype(bf16))
    joint_out = product(att_low, joint_own).astype(bf16).reshape(size, rows, 3 * feats)
    rel_low = product(table_low, rel_own).astype(bf16)
    attended, log_totals = attend(own_at, joint_out, rel_low, bias_rows, key_mask)
    attended_low = jnp.concatenate(
        [attended[0]] + [lay.send(attended[s], lay.to_class(s)) for s in range(1, size)], axis=1
    )
    section_two = section_one + product(attended_low, merge_slots)
    conv_normed, conv_normal, conv_inv = norm_fwd(section_two, gain_rows[2], shift_rows[2])
    conv_low = lay.all_slots(conv_normed.astype(bf16))
    wide_out = product(conv_low, wide_own).reshape(size, rows, 2 * feats)
    lin_half = wide_out[:, :, :feats]
    gate_sig = jax.nn.sigmoid(wide_out[:, :, feats:])
    gated = lin_half * gate_sig * live_col
    framed = framed_rows(gated)
    depth_out = kernel_taps[0] * framed[:, 0:rows]
    for offset in range(1, KW):
        depth_out = depth_out + kernel_taps[offset] * framed[:, offset : offset + rows]
    own_count = length.astype(f32)
    own_mean = jnp.sum(depth_out * live_col, axis=(0, 1)) / own_count
    own_gap = (depth_out - own_mean) * live_col
    moments = jnp.stack(
        [jnp.broadcast_to(own_count, (feats,)), own_mean, jnp.sum(own_gap * own_gap, axis=(0, 1))]
    )
    total_count, bn_mean, total_var = lay.over_utterances(moments, merge_moments)
    bn_inv = lax.rsqrt(total_var / total_count + eps_norm)
    bn_normal = (depth_out - bn_mean) * bn_inv
    bn_flat = bn_normal * batch_gain + batch_shift
    swish_low = (bn_flat * jax.nn.sigmoid(bn_flat)).astype(bf16).reshape(span, feats)
    section_three = section_two + lay.own_sum(product(swish_low, narrow_own))
    section_three, cotangent = lax.optimization_barrier((section_three, cotangent))
    grad_entry = lay.enter(cotangent)
    branch_four, saved_four = feed_forward(
        section_three, gain_rows[3], shift_rows[3], up_two, down_two
    )
    section_four = section_three + 0.5 * branch_four
    final_out, final_normal, final_inv = norm_fwd(section_four, gain_rows[4], shift_rows[4])
    output = lay.leave(final_out.astype(bf16).reshape(utt_count, block_len, D))

    grad_final = grad_entry.astype(f32).reshape(rows, D)
    grad_four, gain_four, shift_four = norm_back(grad_final, final_normal, final_inv, gain_rows[4])

    def scatter_two(grad_down, grad_up, grad_hidden):
        moved = lay.scatter([grad_up, grad_down])
        return grad_hidden, moved

    grad_mid, moved_two, gain_three, shift_three = feed_back(
        0.5 * grad_four, saved_four, gain_rows[3], up_two, down_two, scatter_two
    )
    grad_three = grad_four + grad_mid
    narrow_low = lay.all_slots(grad_three.astype(bf16))
    grad_narrow = lay.sub_place(product_tn(swish_low, narrow_low), 0)
    grad_batch = product_nt(narrow_low, narrow_own).reshape(size, rows, feats) * swish_grad(bn_flat)
    gain_batch = jnp.sum(grad_batch * bn_normal, axis=(0, 1))
    shift_batch = jnp.sum(grad_batch, axis=(0, 1))
    grad_hat = grad_batch * batch_gain
    total_hat, total_cross = lay.over_utterances(
        jnp.stack([shift_batch * batch_gain, gain_batch * batch_gain]), jnp.add
    )
    grad_depth = bn_inv * (
        grad_hat - live_col / total_count * (total_hat + bn_normal * total_cross)
    )
    grad_framed = framed_rows(grad_depth)
    grad_gated = kernel_taps[0] * grad_framed[:, KW - 1 : KW - 1 + rows]
    for offset in range(1, KW):
        grad_gated = (
            grad_gated + kernel_taps[offset] * grad_framed[:, KW - 1 - offset : KW - 1 - offset + rows]
        )
    grad_taps = jnp.stack(
        [
            jnp.sum(grad_depth * framed[:, offset : offset + rows], axis=(0, 1))
            for offset in range(KW)
        ]
    )
    grad_glu = grad_gated * live_col
    grad_wide_out = (
        jnp.concatenate(
            [grad_glu * gate_sig, grad_glu * lin_half * gate_sig * (1.0 - gate_sig)], axis=2
        )
        .astype(bf16)
        .reshape(span, 2 * feats)
    )
    grad_wide = lay.sub_place(product_tn(conv_low, grad_wide_out).reshape(D, 2, feats), 2)
    grad_conv_in, gain_two, shift_two = norm_back(
        lay.own_sum(product_nt(grad_wide_out, wide_own)), conv_normal, conv_inv, gain_rows[2]
    )
    grad_two = grad_three + grad_conv_in
    merge_low, output = lax.optimization_barrier((grad_two.astype(bf16), output))
    grad_merge = product_tn(attended_low, merge_low).astype(bf16)
    grad_merge = jnp.concatenate(
        [
            lax.dynamic_slice_in_dim(grad_merge, (own ^ s) * feats, feats, axis=0)
            for s in range(size)
        ],
        axis=0,
    )
    halves = grad_merge.reshape(D, 2, D // 2)
    mine = lax.dynamic_index_in_dim(halves, lay.core, 1, keepdims=False)
    theirs = lax.dynamic_index_in_dim(halves, 1 - lay.core, 1, keepdims=False)
    grad_merge = mine.astype(f32) + lay.send(theirs, lay.to_core).astype(f32)
    grad_attended = product_nt(merge_low, merge_slots).astype(bf16).reshape(rows, size, feats)
    grad_attended = jnp.stack(
        [grad_attended[:, 0]]
        + [lay.send(grad_attended[:, s], lay.to_class(s)) for s in range(1, size)]
    )
    grad_attended, rows_two = lax.optimization_barrier((grad_attended, moved_two[0]))
    moved_conv = lay.scatter([grad_merge, grad_wide.reshape(D, D), grad_narrow], after=rows_two)
    grad_query, grad_key, grad_value, grad_rel, grad_biases = attend_back(
        own_at, joint_out, rel_low, bias_rows, key_mask, attended, grad_attended, log_totals
    )
    grad_query, rows_conv = lax.optimization_barrier((grad_query, moved_conv[0]))
    grad_biases = grad_biases.transpose(1, 0, 2).reshape(2, feats)
    rel_high = grad_rel.astype(bf16)
    rel_rest = (grad_rel - rel_high.astype(f32)).astype(bf16)
    grad_rel_proj = lay.sub_place(
        product_tn(table_low, rel_high) + product_tn(table_low, rel_rest), 1
    )
    grad_joint_out = jnp.concatenate([grad_query, grad_key, grad_value], axis=2).reshape(
        span, 3 * feats
    )
    grad_joint = lay.sub_place(product_tn(att_low, grad_joint_out).reshape(D, 3, feats), 2)
    grad_att_in, gain_one, shift_one = norm_back(
        lay.own_sum(product_nt(grad_joint_out, joint_own)), att_normal, att_inv, gain_rows[1]
    )
    grad_one = grad_two + grad_att_in
    moved_joint = lay.scatter(
        [grad_joint.reshape(D, 3 * D // 2), grad_rel_proj], over_planes=True, after=rows_conv
    )

    def scatter_one(grad_down, grad_up, grad_hidden):
        grad_hidden, rows_joint = lax.optimization_barrier((grad_hidden, moved_joint[0]))
        moved_down = lay.scatter([grad_down], after=rows_joint)
        moved_up = lay.scatter([grad_up], over_planes=True, after=moved_down[0])
        return grad_hidden, (moved_down, moved_up)

    grad_first, (moved_down, moved_up), gain_zero, shift_zero = feed_back(
        0.5 * grad_one, saved_one, gain_rows[0], up_one, down_one, scatter_one
    )
    grad_zero = grad_one + grad_first
    grad_inputs = lay.leave(grad_zero.astype(bf16).reshape(utt_count, block_len, D))

    summed_up_two, summed_down_two = lay.collect(rows_two, moved_two[1])
    summed_merge, summed_wide, summed_narrow = lay.collect(rows_conv, moved_conv[1])
    summed_joint, summed_rel = lay.collect(*moved_joint)
    (summed_down_one,) = lay.collect(*moved_down)
    (summed_up_one,) = lay.collect(*moved_up)
    summed_up_one = lay.cols_join(summed_up_one, tm)
    summed_up_two = lay.cols_join(summed_up_two, tm)
    summed_joint = lay.cols_join(summed_joint, 3)
    summed_rel = lay.cols_join(summed_rel, 1)
    summed_merge = lay.cols_join(summed_merge, 1)
    summed_wide = lay.cols_join(summed_wide, 2 * tm)
    summed_down_one = summed_down_one.reshape(-1, D)
    summed_down_two = summed_down_two.reshape(-1, D)
    summed_narrow = summed_narrow.reshape(-1, D)

    small_grads = jnp.concatenate(
        [
            jnp.stack([gain_zero, gain_one, gain_two, gain_three, gain_four]),
            place_feats(gain_batch[None]),
            jnp.stack([shift_zero, shift_one, shift_two, shift_three, shift_four]),
            place_feats(shift_batch[None]),
            place_heads(grad_biases),
            place_feats(grad_taps),
        ],
        axis=0,
    )
    small_grads = lay.sum_all(small_grads)
    small_grads = lax.dynamic_slice_in_dim(small_grads, lay.t * (D // tm), D // tm, axis=1)
    return (
        output,
        grad_inputs,
        summed_up_one,
        summed_down_one,
        summed_joint,
        summed_rel,
        summed_merge,
        summed_wide,
        summed_narrow,
        summed_up_two,
        summed_down_two,
        small_grads[0:6],
        small_grads[6:12],
        small_grads[12:14],
        small_grads[14 : 14 + KW],
    )


def solution(mesh):
    frames = P("dp", "tm", None)
    rows, cols = P("tm", None), P(None, "tm")
    return jax.shard_map(
        body,
        mesh=mesh,
        in_specs=(frames, frames, P("dp")) + (rows,) * 9 + (cols,) * 4,
        out_specs=(frames, frames) + (rows,) * 9 + (cols,) * 4,
        check_vma=False,
    )
```

time: 5490 us -> 1370 us (0.25)
  waiting for transfers between devices: 2550 us -> 424 us
  local copies, waits for them, and re-layouts: 1610 us -> 168 us
  matrix products: 847 us -> 262 us
  blocking collectives: 207 us -> 0 us
  Pallas kernels: 0 us -> 195 us
  starting transfers between devices: 26.5 us -> 99.9 us
    reduce_scatter x25 -> x5, waiting for transfers between devices: 1370 us -> 37.5 us  [scatter(): lax.psum_scatter(mine, 'tm', scatter_dimension=0, tiled=True)]
    all_gather x41 -> x4, waiting for transfers between devices: 806 us -> 104 us  [gather(): lax.all_gather(packed[None], AXES, axis=0, tiled=True, axis_index_groups=...]
    reshape x50 -> x14, local copies, waits for them, and re-layouts: 633 us -> 27.3 us  [the longest x10 23.3 us: cols_join(): return split.transpose(1, 2, 0, 3).reshape(rows, 2 * cols)]
    while x144 -> x0, local copies, waits for them, and re-layouts: 567 us -> none
    dot_general x98 -> x9, matrix products: 654 us -> 88.6 us  [product(): return jnp.dot(left, right, preferred_element_type=f32)]
    ppermute x4 -> x65, waiting for transfers between devices: 0.01 us -> 282 us  [the longest x57 201 us: send(): return lax.ppermute(values, AXES, self.route(target))]
    unnamed x27 -> x9, waiting for transfers between devices: 256 us -> 0.15 us
    pallas_call x0 -> x2, Pallas kernels: none -> 195 us  [the longest x1 137 us: attend_back(): pl.pallas_call(functools.partial(attend_back_kernel, slots=slots, rows=ro...]
  transfers between devices with their start and end apart: 75 -> 74, of which waited for: 43 -> 35; matrix products, arithmetic and copies ran while one was open for 40% -> 35% of each run, Pallas kernels for 0% -> 14%
where the time goes in v1:
time: 1370 us; the launch traced here: 1360 us
  waiting for transfers between devices  424 us (31%)
  matrix products  262 us (19%)
  other arithmetic  197 us (14%)
  Pallas kernels  195 us (14%)
  local copies, waits for them, and re-layouts  168 us (12%)
  starting transfers between devices  99.9 us (7%)
  between operations  18.6 us (1%)
    ppermute x57, waiting for transfers between devices, send(): return lax.ppermute(values, AXES, self.route(target))  201 us
    pallas_call x1, Pallas kernels, attend_back(): pl.pallas_call(functools.partial(attend_back_kernel, slots=slots, rows=ro...  137 us
    all_gather x4, waiting for transfers between devices, gather(): lax.all_gather(packed[None], AXES, axis=0, tiled=True, axis_index_groups=...  104 us
    dot_general x9, matrix products, product(): return jnp.dot(left, right, preferred_element_type=f32)  88.6 us
    dot_general x10, matrix products, product_tn(): lax.dot_general(left, right, (((0,), (0,)), ((), ())), preferred_element_...  87.3 us
    dot_general x8, matrix products, product_nt(): lax.dot_general(left, right, (((1,), (1,)), ((), ())), preferred_element_...  86.6 us
    ppermute x8, waiting for transfers between devices, leave(): block = lax.ppermute(block, AXES, [(b, a) for a, b in there])  81.3 us
    ppermute x57, starting transfers between devices, send(): return lax.ppermute(values, AXES, self.route(target))  75.5 us
  transfers between devices with their start and end apart: 74, of which 35 were waited for; matrix products, arithmetic and copies ran while one was open for 35% of the time, Pallas kernels for 14%

profile of v1, /device:TPU:11, one launch (start us, length us, event | category | flops | bytes accessed | tf_op | source)
XLA Modules:
  0.0 1365.0 jit_solution(838738310591689730)
XLA Ops:
  43.4 25.0 %collective-permute-done.5 = bf16[2,19,128]{2,1,0:T(8,128)(2,1)S(1)} collective-permute-done((bf16[2,19,128]{2,1,0:T(8,128)(2,1)S(1)}, bf16[2,19,128]{2,1,0:T(8,128)(2,1)S(1)}, u32[]{:S(2)}, u32[]{:S(2)}) %collective-permute-start.5) | collective-permute-done | bytes 9760 | tf_op jit(solution)/shard_map/ppermute | solution.py:272
  73.3 18.7 %collective-permute-done.6 = bf16[4,19,128]{2,1,0:T(8,128)(2,1)S(1)} collective-permute-done((bf16[4,19,128]{2,1,0:T(8,128)(2,1)S(1)}, bf16[4,19,128]{2,1,0:T(8,128)(2,1)S(1)}, u32[]{:S(2)}, u32[]{:S(2)}) %collective-permute-start.6) | collective-permute-done | bytes 19488 | tf_op jit(solution)/shard_map/ppermute | solution.py:272
  104.2 32.8 %fusion = (bf16[4096,512]{1,0:T(8,128)(2,1)}, bf16[4096,512]{1,0:T(8,128)(2,1)}) fusion(f32[512]{0:T(512)S(1)} %multiply_exponential_fusion, f32[4096]{0:T(1024)S(1)} %subtract_convert_fusion.4), kind=kLoop, calls=%fused_computation.9 | loop fusion | flops 6291456 | bytes 8407040 | tf_op jit(solution)/shard_map/convert.37
  145.0 15.8 %all-gather.9.cloned.1.call-done = bf16[4096,1024]{1,0:T(8,128)(2,1)} async-done(((bf16[256,1024]{1,0:T(8,128)(2,1)}), bf16[4096,1024]{1,0:T(8,128)(2,1)}) %all-gather.9.cloned.1.call-update) | async-done | bytes 8388624 | tf_op jit(solution)/shard_map/all_gather | solution.py:396
  166.6 19.5 %multiply_convert_fusion.3 = (bf16[2048,2048]{1,0:T(8,128)(2,1)}, f32[2048,2048]{1,0:T(8,128)}) fusion(bf16[1024,2048]{1,0:T(8,128)(2,1)S(1)} %bitcast.386, bf16[1024,1024]{1,0:T(8,128)(2,1)} %collective-permute-done.7, bf16[1024,1024]{1,0:T(8,128)(2,1)} %fusion.35), kind=kOutput, calls=%fused_computation.5 | convolution fusion | flops 8619294720 | bytes 33554432 | tf_op jit(solution)/shard_map/dot_general | solution.py:25
  212.4 38.4 %all-gather.11.cloned.1.call-done = bf16[2048,1024]{0,1:T(8,128)(2,1)} async-done(((bf16[128,1024]{0,1:T(8,128)(2,1)}), bf16[2048,1024]{0,1:T(8,128)(2,1)}) %all-gather.11.cloned.1.call-update) | async-done | bytes 4194320 | tf_op jit(solution)/shard_map/all_gather | solution.py:396
  287.4 58.5 %attend.1 = (bf16[2,1024,512]{2,1,0:T(8,128)(2,1)}, f32[4,2048,1]{2,1,0:T(8,128)}) custom-call(s32[1]{0:T(128)} %bitcast.13.own_ref, bf16[2,1024,1536]{2,1,0:T(8,128)(2,1)} %bitcast.502, bf16[2,1024,1536]{2,1,0:T(8,128)(2,1)} %bitcast.503, bf16[2,1024,1536]{2,1,0:T(8,128)(2,1)} %bitcast.504, bf16[4096,512]{1,0:T(8,128)(2,1)} %convolution_convert_fusion.1.rel_ref, ...), custom_call_target="tpu_custom_call" | custom-call | flops 17179869184 | bytes 20971520 | tf_op jit(solution)/shard_map/attend/pallas_call | solution.py:161
  426.2 50.0 %all-gather.15.cloned.1.call-done = bf16[4096,1024]{1,0:T(8,128)(2,1)} async-done(((bf16[256,1024]{1,0:T(8,128)(2,1)}), bf16[4096,1024]{1,0:T(8,128)(2,1)}) %all-gather.15.cloned.1.call-update) | async-done | bytes 8388624 | tf_op jit(solution)/shard_map/all_gather | solution.py:396
  482.0 19.0 %multiply_convert_fusion.2 = (bf16[2048,2048]{1,0:T(8,128)(2,1)}, f32[2048,2048]{1,0:T(8,128)}) fusion(bf16[1024,2048]{1,0:T(8,128)(2,1)S(1)} %bitcast.392, bf16[1024,1024]{1,0:T(8,128)(2,1)} %collective-permute-done.18, bf16[1024,1024]{1,0:T(8,128)(2,1)S(1)} %add_convert_fusion.3), kind=kOutput, calls=%fused_computation.3 | convolution fusion | flops 8619294720 | bytes 33554432 | tf_op jit(solution)/shard_map/dot_general | solution.py:25
  524.9 26.5 %collective-permute-done.20 = bf16[1,256,1024]{2,1,0:T(8,128)(2,1)S(1)} collective-permute-done((bf16[1,256,1024]{2,1,0:T(8,128)(2,1)S(1)}, bf16[1,256,1024]{2,1,0:T(8,128)(2,1)S(1)}, u32[]{:S(2)}, u32[]{:S(2)}) %collective-permute-start.20) | collective-permute-done | bytes 524320 | tf_op jit(solution)/shard_map/ppermute | solution.py:272
  551.7 14.0 %collective-permute-done.21 = bf16[1,256,1024]{2,1,0:T(8,128)(2,1)S(1)} collective-permute-done((bf16[1,256,1024]{2,1,0:T(8,128)(2,1)S(1)}, bf16[1,256,1024]{2,1,0:T(8,128)(2,1)S(1)}, u32[]{:S(2)}, u32[]{:S(2)}) %collective-permute-start.21) | collective-permute-done | bytes 524320 | tf_op jit(solution)/shard_map/ppermute | solution.py:272
  593.1 20.1 %multiply_convert_fusion.1 = bf16[2048,2048]{1,0:T(8,128)(2,1)} fusion(f32[2048,2048]{1,0:T(8,128)} %get-tuple-element.314, bf16[2048,1024]{1,0:T(8,128)(2,1)} %pad_maximum_fusion.12, bf16[2048,1024]{1,0:T(8,128)(2,1)S(1)} %bitcast.391), kind=kOutput, calls=%fused_computation.2 | convolution fusion | flops 8627683328 | bytes 33554432 | tf_op jit(solution)/shard_map/dot_general | solution.py:29
  613.3 12.5 fusion.138
  631.1 13.3 convolution_convert_fusion.4
  730.6 23.9 %collective-permute-done.32 = bf16[1,256,1024]{2,1,0:T(8,128)(2,1)} collective-permute-done((bf16[1,256,1024]{2,1,0:T(8,128)(2,1)}, bf16[1,256,1024]{2,1,0:T(8,128)(2,1)}, u32[]{:S(2)}, u32[]{:S(2)}) %collective-permute-start.32) | collective-permute-done | bytes 524320 | tf_op jit(solution)/shard_map/ppermute | solution.py:311
  758.0 17.6 %collective-permute-done.33 = bf16[1,256,1024]{2,1,0:T(8,128)(2,1)} collective-permute-done((bf16[1,256,1024]{2,1,0:T(8,128)(2,1)}, bf16[1,256,1024]{2,1,0:T(8,128)(2,1)}, u32[]{:S(2)}, u32[]{:S(2)}) %collective-permute-start.33) | collective-permute-done | bytes 524320 | tf_op jit(solution)/shard_map/ppermute | solution.py:311
  846.0 136.7 %attend_back.1 = (bf16[2,1024,512]{2,1,0:T(8,128)(2,1)}, bf16[2,1024,512]{2,1,0:T(8,128)(2,1)}, bf16[2,1024,512]{2,1,0:T(8,128)(2,1)}, f32[4096,512]{1,0:T(8,128)}, f32[4,2,128]{2,1,0:T(2,128)}) custom-call(s32[1]{0:T(128)} %bitcast.13.own_ref, bf16[2,1024,1536]{2,1,0:T(8,128)(2,1)} %bitcast.505, bf16[2,1024,1536]{2,1,0:T(8,128)(2,1)} %bitcast.506, ...), custom_call_target="tpu_custom_call" | custom-call | flops 47244640256 | bytes 41943040 | tf_op jit(solution)/shard_map/attend_back/pallas_call | solution.py:190
  1041.2 42.1 %collective-permute-done.55 = bf16[1,160,1024]{2,1,0:T(8,128)(2,1)S(1)} collective-permute-done((bf16[1,160,1024]{2,1,0:T(8,128)(2,1)S(1)}, bf16[1,160,1024]{2,1,0:T(8,128)(2,1)S(1)}, u32[]{:S(2)}, u32[]{:S(2)}) %collective-permute-start.55) | collective-permute-done | bytes 327712 | tf_op jit(solution)/shard_map/ppermute | solution.py:272
  1117.8 20.7 %multiply_convert_fusion = bf16[2048,2048]{1,0:T(8,128)(2,1)} fusion(f32[2048,2048]{1,0:T(8,128)} %get-tuple-element.310, bf16[2048,1024]{1,0:T(8,128)(2,1)} %pad_maximum_fusion.15, bf16[2048,1024]{1,0:T(8,128)(2,1)} %bitcast.389), kind=kOutput, calls=%fused_computation.1 | convolution fusion | flops 8627683328 | bytes 33554432 | tf_op jit(solution)/shard_map/dot_general | solution.py:29
  1138.5 12.8 convolution_convert_fusion.3
  1155.1 12.7 fusion.140
  1183.9 24.0 %collective-permute-done.52 = bf16[1,128,1024]{2,1,0:T(8,128)(2,1)S(1)} collective-permute-done((bf16[1,128,1024]{2,1,0:T(8,128)(2,1)S(1)}, bf16[1,128,1024]{2,1,0:T(8,128)(2,1)S(1)}, u32[]{:S(2)}, u32[]{:S(2)}) %collective-permute-start.52) | collective-permute-done | bytes 262176 | tf_op jit(solution)/shard_map/ppermute | solution.py:272
  1215.1 29.0 %reduce-scatter.12.cloned.1.call-done = bf16[1,2,128,1024]{3,2,1,0:T(8,128)(2,1)} async-done(((bf16[8,2,128,1024]{3,2,1,0:T(8,128)(2,1)}), bf16[1,2,128,1024]{3,2,1,0:T(8,128)(2,1)}) %reduce-scatter.12.cloned.1.call-update) | async-done | bytes 524304 | tf_op jit(solution)/shard_map/reduce_scatter | solution.py:415
  1307.7 13.1 collective-permute-done.43
  (820 shorter events, 649.5 us)
Async XLA Ops:
  7.2 153.6 %all-gather.9.cloned.1.call-start = ((), (), s32[]{:S(2)}) async-start(), calls=%async_computation.10 | async-start | bytes 8912896 | tf_op jit(solution)/shard_map/all_gather | solution.py:396
  17.5 233.3 %all-gather.11.cloned.1.call-start = ((), (), s32[]{:S(2)}) async-start(), calls=%async_computation.11 | async-start | bytes 4456448 | tf_op jit(solution)/shard_map/all_gather | solution.py:396
  19.0 74.9 %collective-permute-start = (bf16[1,256,1024]{2,1,0:T(8,128)(2,1)}, bf16[1,256,1024]{2,1,0:T(8,128)(2,1)}, u32[]{:S(2)}, u32[]{:S(2)}) collective-permute-start(bf16[1,256,1024]{2,1,0:T(8,128)(2,1)} %get-tuple-element.236), channel_id=1, source_target_pairs={{0,0},{1,2},{2,4},{3,6},{4,8},{5,10},{6,12},{7,14},{8,1},{9,3},{10... | collective-permute-start | bytes 1572872 | tf_op jit(solution)/shard_map/ppermute | solution.py:272
  23.8 71.5 %collective-permute-start.1 = (bf16[1,256,1024]{2,1,0:T(8,128)(2,1)}, bf16[1,256,1024]{2,1,0:T(8,128)(2,1)}, u32[]{:S(2)}, u32[]{:S(2)}) collective-permute-start(bf16[1,256,1024]{2,1,0:T(8,128)(2,1)} %get-tuple-element.235), channel_id=1, source_target_pairs={{0,2},{1,4},{2,6},{3,0},{4,10},{5,12},{6,14},{7,8},{8,3},{9,5},{10... | collective-permute-start | bytes 1572872 | tf_op jit(solution)/shard_map/ppermute | solution.py:272
  25.7 70.7 %collective-permute-start.2 = (bf16[1,256,1024]{2,1,0:T(8,128)(2,1)}, bf16[1,256,1024]{2,1,0:T(8,128)(2,1)}, u32[]{:S(2)}, u32[]{:S(2)}) collective-permute-start(bf16[1,256,1024]{2,1,0:T(8,128)(2,1)} %get-tuple-element.237), channel_id=1, source_target_pairs={{0,4},{1,6},{2,0},{3,2},{4,12},{5,14},{6,8},{7,10},{8,5},{9,7},{10... | collective-permute-start | bytes 1572872 | tf_op jit(solution)/shard_map/ppermute | solution.py:272
  26.1 71.4 %collective-permute-start.3 = (bf16[1,256,1024]{2,1,0:T(8,128)(2,1)}, bf16[1,256,1024]{2,1,0:T(8,128)(2,1)}, u32[]{:S(2)}, u32[]{:S(2)}) collective-permute-start(bf16[1,256,1024]{2,1,0:T(8,128)(2,1)} %get-tuple-element.234), channel_id=1, source_target_pairs={{0,6},{1,0},{2,2},{3,4},{4,14},{5,8},{6,10},{7,12},{8,7},{9,1},{10... | collective-permute-start | bytes 1572872 | tf_op jit(solution)/shard_map/ppermute | solution.py:272
  35.4 315.4 %all-gather.13.cloned.1.call-start = ((), (), s32[]{:S(2)}) async-start(), calls=%async_computation.12 | async-start | bytes 5570560 | tf_op jit(solution)/shard_map/all_gather | solution.py:396
  101.9 64.7 %collective-permute-start.7 = (bf16[1024,1024]{1,0:T(8,128)(2,1)}, bf16[1024,1024]{1,0:T(8,128)(2,1)}, u32[]{:S(2)}, u32[]{:S(2)}) collective-permute-start(bf16[1024,1024]{1,0:T(8,128)(2,1)} %fusion.35), channel_id=1, source_target_pairs={{0,8},{1,9},{2,10},{3,11},{4,12},{5,13},{6,14},{7,15},{8,0},{9,1},... | collective-permute-start | bytes 6291464 | tf_op jit(solution)/shard_map/ppermute | solution.py:272
  202.9 56.1 %collective-permute-start.8 = (bf16[1024,1024]{1,0:T(8,128)(2,1)}, bf16[1024,1024]{1,0:T(8,128)(2,1)}, u32[]{:S(2)}, u32[]{:S(2)}) collective-permute-start(bf16[1024,1024]{1,0:T(8,128)(2,1)} %slice.795), channel_id=1, source_target_pairs={{0,8},{1,9},{2,10},{3,11},{4,12},{5,13},{6,14},{7,15},{8,0},{9,1},... | collective-permute-start | bytes 6291464 | tf_op jit(solution)/shard_map/ppermute | solution.py:272
  208.7 267.5 %all-gather.15.cloned.1.call-start = ((), (), s32[]{:S(2)}) async-start(), calls=%async_computation.13 | async-start | bytes 8912896 | tf_op jit(solution)/shard_map/all_gather | solution.py:396
  364.7 477.1 %reduce-scatter.6.cloned.1.call-start = ((), (), s32[]{:S(2)}) async-start(), calls=%async_computation.5 | async-start | bytes 9437184 | tf_op jit(solution)/shard_map/reduce_scatter | solution.py:415
  425.8 56.2 %collective-permute-start.18 = (bf16[1024,1024]{1,0:T(8,128)(2,1)S(1)}, bf16[1024,1024]{1,0:T(8,128)(2,1)}, u32[]{:S(2)}, u32[]{:S(2)}) collective-permute-start(bf16[1024,1024]{1,0:T(8,128)(2,1)S(1)} %add_convert_fusion.3), channel_id=1, source_target_pairs={{0,8},{1,9},{2,10},{3,11},{4,12},{5,13},{6,14},{7,15},{8,0},{9,1},... | collective-permute-start | bytes 6291464 | tf_op jit(solution)/shard_map/ppermute | solution.py:272
  512.6 54.9 %collective-permute-start.19 = (bf16[1024,1024]{1,0:T(8,128)(2,1)S(1)}, bf16[1024,1024]{1,0:T(8,128)(2,1)}, u32[]{:S(2)}, u32[]{:S(2)}) collective-permute-start(bf16[1024,1024]{1,0:T(8,128)(2,1)S(1)} %slice.793), channel_id=1, source_target_pairs={{0,8},{1,9},{2,10},{3,11},{4,12},{5,13},{6,14},{7,15},{8,0},{9,1},... | collective-permute-start | bytes 6291464 | tf_op jit(solution)/shard_map/ppermute | solution.py:272
  666.0 341.4 %reduce-scatter.8.cloned.1.call-start = ((), (), s32[]{:S(2)}) async-start(), calls=%async_computation.6 | async-start | bytes 5898240 | tf_op jit(solution)/shard_map/reduce_scatter | solution.py:415
  714.0 81.5 %collective-permute-start.31 = (bf16[1024,1024]{1,0:T(8,128)(2,1)}, bf16[1024,1024]{1,0:T(8,128)(2,1)S(1)}, u32[]{:S(2)}, u32[]{:S(2)}) collective-permute-start(bf16[1024,1024]{1,0:T(8,128)(2,1)} %slice.791), channel_id=1, source_target_pairs={{0,8},{1,9},{2,10},{3,11},{4,12},{5,13},{6,14},{7,15},{8,0},{9,1},... | collective-permute-start | bytes 6291464 | tf_op jit(solution)/shard_map/ppermute | solution.py:272
  728.5 60.3 %collective-permute-start.35 = (bf16[1,256,1024]{2,1,0:T(8,128)(2,1)}, bf16[1,256,1024]{2,1,0:T(8,128)(2,1)S(1)}, u32[]{:S(2)}, u32[]{:S(2)}) collective-permute-start(bf16[1,256,1024]{2,1,0:T(8,128)(2,1)} %get-tuple-element.222), channel_id=1, source_target_pairs={{6,0},{0,1},{2,2},{4,3},{14,4},{8,5},{10,6},{12,7},{7,8},{1,9},{3,... | collective-permute-start | bytes 1572872 | tf_op jit(solution)/shard_map/ppermute | solution.py:311
  841.8 313.3 %reduce-scatter.10.cloned.1.call-start = ((), (), s32[]{:S(2)}) async-start(), calls=%async_computation.7 | async-start | bytes 2359296 | tf_op jit(solution)/shard_map/reduce_scatter | solution.py:415
  844.8 147.8 %collective-permute-start.57 = (bf16[1,256,1024]{2,1,0:T(8,128)(2,1)S(1)}, bf16[1,256,1024]{2,1,0:T(8,128)(2,1)S(1)}, u32[]{:S(2)}, u32[]{:S(2)}) collective-permute-start(bf16[1,256,1024]{2,1,0:T(8,128)(2,1)S(1)} %slice_bitcast_fusion.2), channel_id=1, source_target_pairs={{0,16},{1,17},{2,18},{3,19},{4,20},{5,21},{6,22},{7,23},{8,24},{9,... | collective-permute-start | bytes 1572872 | tf_op jit(solution)/shard_map/ppermute | solution.py:272
  1029.1 55.9 %collective-permute-start.40 = (bf16[8,128,1024]{2,1,0:T(8,128)(2,1)S(1)}, bf16[8,128,1024]{2,1,0:T(8,128)(2,1)S(1)}, u32[]{:S(2)}, u32[]{:S(2)}) collective-permute-start(bf16[8,128,1024]{2,1,0:T(8,128)(2,1)S(1)} %maximum_maximum_fusion.2), channel_id=1, source_target_pairs={{0,16},{1,17},{2,18},{3,19},{4,20},{5,21},{6,22},{7,23},{8,24},{9,... | collective-permute-start | bytes 6291464 | tf_op jit(solution)/shard_map/ppermute | solution.py:272
  1039.0 59.7 %collective-permute-start.39 = (bf16[1024,1024]{1,0:T(8,128)(2,1)}, bf16[1024,1024]{1,0:T(8,128)(2,1)}, u32[]{:S(2)}, u32[]{:S(2)}) collective-permute-start(bf16[1024,1024]{1,0:T(8,128)(2,1)} %get-tuple-element.153), channel_id=1, source_target_pairs={{0,8},{1,9},{2,10},{3,11},{4,12},{5,13},{6,14},{7,15},{8,0},{9,1},... | collective-permute-start | bytes 6291464 | tf_op jit(solution)/shard_map/ppermute | solution.py:272
  1087.2 156.8 %reduce-scatter.12.cloned.1.call-start = ((), (), s32[]{:S(2)}) async-start(), calls=%async_computation.8 | async-start | bytes 4718592 | tf_op jit(solution)/shard_map/reduce_scatter | solution.py:415
  1117.8 211.6 %reduce-scatter.14.cloned.1.call-start = ((), (), s32[]{:S(2)}) async-start(), calls=%async_computation.9 | async-start | bytes 2359296 | tf_op jit(solution)/shard_map/reduce_scatter | solution.py:415
  1154.7 56.4 %collective-permute-start.46 = (bf16[8,128,1024]{2,1,0:T(8,128)(2,1)}, bf16[8,128,1024]{2,1,0:T(8,128)(2,1)}, u32[]{:S(2)}, u32[]{:S(2)}) collective-permute-start(bf16[8,128,1024]{2,1,0:T(8,128)(2,1)} %pad_maximum_fusion.30), channel_id=1, source_target_pairs={{0,16},{1,17},{2,18},{3,19},{4,20},{5,21},{6,22},{7,23},{8,24},{9,... | collective-permute-start | bytes 6291464 | tf_op jit(solution)/shard_map/ppermute | solution.py:272
  1172.9 74.2 %collective-permute-start.41 = (bf16[1024,1024]{1,0:T(8,128)(2,1)}, bf16[1024,1024]{1,0:T(8,128)(2,1)}, u32[]{:S(2)}, u32[]{:S(2)}) collective-permute-start(bf16[1024,1024]{1,0:T(8,128)(2,1)} %slice.789), channel_id=1, source_target_pairs={{0,8},{1,9},{2,10},{3,11},{4,12},{5,13},{6,14},{7,15},{8,0},{9,1},... | collective-permute-start | bytes 6291464 | tf_op jit(solution)/shard_map/ppermute | solution.py:272
  (213 other events, 3161.2 us)
Sparse Core Ops, SparseCore 0:
  17.6 143.1 all-gather.8
  164.1 86.6 all-gather.10
  254.2 84.7 all-gather.12
  364.8 111.3 all-gather.14
  666.1 172.3 reduce-scatter.5
  842.4 102.9 reduce-scatter.7
  1087.3 63.5 reduce-scatter.9
  1155.0 89.0 reduce-scatter.11
  1248.2 81.1 reduce-scatter.13

commit v2 on v1

--- a/solution.py
+++ b/solution.py
@@ -138,60 +138,74 @@
         drel_ref[...] = drel_ref[...] * (1.0 / LOG2E)
 
 
-def attention_specs(slots, rows, heads, tile):
+def attention_specs(slots, rows, heads, tile, first):
     per = rows // tile
     span = slots * rows
-    by_tile = pl.BlockSpec((1, tile, HEAD_DIM), lambda h, i, own: (i // per, i % per, h))
+    by_tile = pl.BlockSpec((1, tile, HEAD_DIM), lambda h, i, own: (i // per, i % per, first + h))
     in_specs = [
         by_tile,
-        pl.BlockSpec((slots, rows, HEAD_DIM), lambda h, i, own: (0, 0, heads + h)),
-        pl.BlockSpec((slots, rows, HEAD_DIM), lambda h, i, own: (0, 0, 2 * heads + h)),
-        pl.BlockSpec((2 * span, HEAD_DIM), lambda h, i, own: (0, h)),
-        pl.BlockSpec((2, HEAD_DIM), lambda h, i, own: (0, h)),
+        pl.BlockSpec((slots, rows, HEAD_DIM), lambda h, i, own: (0, 0, heads + first + h)),
+        pl.BlockSpec((slots, rows, HEAD_DIM), lambda h, i, own: (0, 0, 2 * heads + first + h)),
+        pl.BlockSpec((2 * span, HEAD_DIM), lambda h, i, own: (0, first + h)),
+        pl.BlockSpec((2, HEAD_DIM), lambda h, i, own: (0, first + h)),
         pl.BlockSpec((1, span), lambda h, i, own: (0, 0)),
     ]
-    return (heads, slots * per), by_tile, in_specs
-
-
-def attend(own, joint, rel, bias, mask):
+    return slots * per, by_tile, in_specs
+
+
+def attend(own, joint, rel, bias, mask, first, count, before=None):
     slots, rows, wide = joint.shape
     heads = wide // (3 * HEAD_DIM)
     span, tile = slots * rows, min(256, rows)
-    grid, by_tile, in_specs = attention_specs(slots, rows, heads, tile)
+    tiles, by_tile, in_specs = attention_specs(slots, rows, heads, tile, first)
+    by_row = pl.BlockSpec((1, tile, 1), lambda h, i, own: (first + h, i, 0))
+    kernel = functools.partial(attend_kernel, slots=slots, rows=rows, tile=tile)
+    operands, aliases = (own, joint, joint, joint, rel, bias, mask), {}
+    if before is not None:
+        operands += tuple(before)
+        in_specs = in_specs + [pl.BlockSpec(memory_space=pl.ANY)] * 2
+        aliases = {7: 0, 8: 1}
+
+        def body_kernel(*refs):
+            kernel(*refs[:7], *refs[9:])
+
+    else:
+        body_kernel = kernel
     return pl.pallas_call(
-        functools.partial(attend_kernel, slots=slots, rows=rows, tile=tile),
+        body_kernel,
         grid_spec=pltpu.PrefetchScalarGridSpec(
             num_scalar_prefetch=1,
-            grid=grid,
+            grid=(count, tiles),
             in_specs=in_specs,
-            out_specs=[by_tile, pl.BlockSpec((1, tile, 1), lambda h, i, own: (h, i, 0))],
+            out_specs=[by_tile, by_row],
             scratch_shapes=[pltpu.VMEM((slots, tile, rows), f32)],
         ),
         out_shape=[
             jax.ShapeDtypeStruct((slots, rows, heads * HEAD_DIM), bf16),
             jax.ShapeDtypeStruct((heads, span, 1), f32),
         ],
+        input_output_aliases=aliases,
         compiler_params=pltpu.CompilerParams(vmem_limit_bytes=56 << 20),
         cost_estimate=pl.CostEstimate(
-            flops=heads * span * span * HEAD_DIM * 8,
-            bytes_accessed=heads * span * HEAD_DIM * 20,
-            transcendentals=heads * span * span,
+            flops=count * span * span * HEAD_DIM * 20,
+            bytes_accessed=count * span * HEAD_DIM * 20,
+            transcendentals=count * span * span,
         ),
         name="attend",
-    )(own, joint, joint, joint, rel, bias, mask)
+    )(*operands)
 
 
 def attend_back(own, joint, rel, bias, mask, out, grad_out, lse):
     slots, rows, wide = joint.shape
     heads = wide // (3 * HEAD_DIM)
     span, tile = slots * rows, min(256, rows)
-    grid, by_tile, in_specs = attention_specs(slots, rows, heads, tile)
+    tiles, by_tile, in_specs = attention_specs(slots, rows, heads, tile, 0)
     by_head = pl.BlockSpec((slots, rows, HEAD_DIM), lambda h, i, own: (0, 0, h))
     return pl.pallas_call(
         functools.partial(attend_back_kernel, slots=slots, rows=rows, tile=tile),
         grid_spec=pltpu.PrefetchScalarGridSpec(
             num_scalar_prefetch=1,
-            grid=grid,
+            grid=(heads, tiles),
             in_specs=in_specs
             + [by_tile, by_tile, pl.BlockSpec((1, tile, 1), lambda h, i, own: (h, i, 0))],
             out_specs=[
@@ -210,7 +224,7 @@
         ],
         compiler_params=pltpu.CompilerParams(vmem_limit_bytes=56 << 20),
         cost_estimate=pl.CostEstimate(
-            flops=heads * span * span * HEAD_DIM * 22,
+            flops=heads * span * span * HEAD_DIM * 50,
             bytes_accessed=heads * span * HEAD_DIM * 40,
             transcendentals=heads * span * span,
         ),
@@ -289,26 +303,33 @@
 
         return target
 
-    def enter(self, shard):
-        at = self.t % self.utt
-        result = jnp.zeros_like(shard)
-        for k in range(self.utt):
-            block = lax.dynamic_index_in_dim(shard, (k + at) % self.utt, 0, keepdims=True)
-            block = self.send(block, self.home(k))
+    def enter(self, shard, step):
+        at = (step + self.t % self.utt) % self.utt
+        block = lax.dynamic_index_in_dim(shard, at, 0, keepdims=True)
+        return self.send(block, self.home(step))
+
+    def entered(self, blocks):
+        result = jnp.zeros((self.utt,) + blocks[0].shape[1:], blocks[0].dtype)
+        for k, block in enumerate(blocks):
             result = lax.dynamic_update_slice_in_dim(
                 result, block, (self.home_slot - k) % self.utt, axis=0
             )
         return result
 
     def leave(self, blocks):
-        at = self.t % self.utt
-        result = jnp.zeros_like(blocks)
+        received = []
         for k in range(self.utt):
             block = lax.dynamic_index_in_dim(
                 blocks, (self.home_slot - k) % self.utt, 0, keepdims=True
             )
             there = self.route(self.home(k))
-            block = lax.ppermute(block, AXES, [(b, a) for a, b in there])
+            received.append(lax.ppermute(block, AXES, [(b, a) for a, b in there]))
+        return received
+
+    def left(self, received):
+        at = self.t % self.utt
+        result = jnp.zeros((self.utt,) + received[0].shape[1:], received[0].dtype)
+        for k, block in enumerate(received):
             result = lax.dynamic_update_slice_in_dim(result, block, (k + at) % self.utt, axis=0)
         return result
 
@@ -385,10 +406,12 @@
             step *= 2
         return self.over_utterances(values, jnp.add)
 
-    def gather(self, locals_):
+    def gather(self, locals_, ready=None):
         plane = lax.axis_index("dp") // 2
         parts = [lax.dynamic_slice_in_dim(v, plane * (v.shape[0] // self.pairs), v.shape[0] // self.pairs, 0) for v in locals_]
         packed, places = pack(parts)
+        if ready is not None:
+            ready.append(packed)
         groups = [
             [(2 * p + c) * self.tm + t for t in range(self.tm) for p in range(self.pairs)]
             for c in range(2)
@@ -508,10 +531,6 @@
     feats = D // size
     pad_width = KW // 2
 
-    small = jnp.concatenate([norm_gains, norm_shifts, pos_biases, depth_taps], axis=0)
-    small = lay.gather_small(small).astype(f32)
-    gain_rows, shift_rows = small[0:6], small[6:12]
-
     def own_feats(values):
         count = values.shape[0]
         split = values.reshape(count, tm, 2, D // (2 * tm))
@@ -529,30 +548,40 @@
             jnp.zeros((values.shape[0], D), f32), values, own * feats, axis=1
         )
 
+    ready = []
+    up_one, down_one, joint_half, rel_half = lay.gather(
+        [
+            lay.cols_half(first_up, tm),
+            lay.core_half(first_down, 0),
+            lay.cols_half(joint_proj, 3),
+            lay.cols_half(rel_proj, 1),
+        ],
+        ready,
+    )
+    _, inputs, norm_gains = lax.optimization_barrier((ready[0], inputs, norm_gains))
+    small = jnp.concatenate([norm_gains, norm_shifts, pos_biases, depth_taps], axis=0)
+    small = lay.gather_small(small).astype(f32)
+    gain_rows, shift_rows = small[0:6], small[6:12]
+
     bias_rows = lax.dynamic_slice_in_dim(small[12:14], own * feats, feats, axis=1)
     kernel_taps = own_feats(small[14 : 14 + KW])
     batch_gain, batch_shift = own_feats(gain_rows[5:6])[0], own_feats(shift_rows[5:6])[0]
 
-    up_one, down_one = lay.gather([lay.cols_half(first_up, tm), lay.core_half(first_down, 0)])
-    joint_half, rel_half = lay.gather([lay.cols_half(joint_proj, 3), lay.cols_half(rel_proj, 1)])
-    merge_full, wide_half, narrow_half = lay.gather(
-        [merge_proj, lay.cols_half(conv_wide, 2 * tm), lay.core_half(conv_narrow, 0)]
-    )
-    up_two, down_two = lay.gather([lay.cols_half(second_up, tm), lay.core_half(second_down, 0)])
+    merge_full, wide_half, narrow_half, up_two, down_two = lay.gather(
+        [
+            merge_proj,
+            lay.cols_half(conv_wide, 2 * tm),
+            lay.core_half(conv_narrow, 0),
+            lay.cols_half(second_up, tm),
+            lay.core_half(second_down, 0),
+        ]
+    )
     up_one, down_one = lay.sub_part(up_one, 1), lay.sub_part(down_one, 0)
     up_two, down_two = lay.sub_part(up_two, 1), lay.sub_part(down_two, 0)
     joint_own = lay.sub_part(joint_half.reshape(D, 3, D // 2), 2).reshape(D, 3 * feats)
     rel_own = lay.sub_part(rel_half, 1)
     wide_own = lay.sub_part(wide_half.reshape(D, 2, D // 2), 2).reshape(D, 2 * feats)
     narrow_own = lay.sub_part(narrow_half, 0)
-    merge_slots = jnp.concatenate(
-        [
-            lax.dynamic_slice_in_dim(merge_full, (own ^ s) * feats, feats, axis=0)
-            for s in range(size)
-        ],
-        axis=0,
-    )
-
     def feed_forward(values, gain_row, shift_row, up_weight, down_weight):
         normed, normal, scale_inv = norm_fwd(values, gain_row, shift_row)
         normed_low = lay.all_slots(normed.astype(bf16))
@@ -604,7 +633,8 @@
     distance = (span - 1 - jnp.arange(2 * span, dtype=jnp.int32)).astype(f32)
     table_low = sinusoid(distance, D).astype(bf16)
     up_one, table_low = lax.optimization_barrier((up_one, table_low))
-    section_zero = lay.enter(inputs).astype(f32).reshape(rows, D)
+    steps = range(utt_count)
+    section_zero = lay.entered([lay.enter(inputs, k) for k in steps]).astype(f32).reshape(rows, D)
     branch_one, saved_one = feed_forward(
         section_zero, gain_rows[0], shift_rows[0], up_one, down_one
     )
@@ -613,7 +643,18 @@
     att_low = lay.all_slots(att_normed.astype(bf16))
     joint_out = product(att_low, joint_own).astype(bf16).reshape(size, rows, 3 * feats)
     rel_low = product(table_low, rel_own).astype(bf16)
-    attended, log_totals = attend(own_at, joint_out, rel_low, bias_rows, key_mask)
+    heads = feats // HEAD_DIM
+    attended, log_totals = attend(own_at, joint_out, rel_low, bias_rows, key_mask, 0, heads)
+
+    merge_full, cotangent = lax.optimization_barrier((merge_full, cotangent))
+    entries = [lay.enter(cotangent, k) for k in steps]
+    merge_slots = jnp.concatenate(
+        [
+            lax.dynamic_slice_in_dim(merge_full, (own ^ s) * feats, feats, axis=0)
+            for s in range(size)
+        ],
+        axis=0,
+    )
     attended_low = jnp.concatenate(
         [attended[0]] + [lay.send(attended[s], lay.to_class(s)) for s in range(1, size)], axis=1
     )
@@ -634,29 +675,28 @@
     moments = jnp.stack(
         [jnp.broadcast_to(own_count, (feats,)), own_mean, jnp.sum(own_gap * own_gap, axis=(0, 1))]
     )
+    moments, entries = lax.optimization_barrier((moments, entries))
     total_count, bn_mean, total_var = lay.over_utterances(moments, merge_moments)
     bn_inv = lax.rsqrt(total_var / total_count + eps_norm)
     bn_normal = (depth_out - bn_mean) * bn_inv
     bn_flat = bn_normal * batch_gain + batch_shift
     swish_low = (bn_flat * jax.nn.sigmoid(bn_flat)).astype(bf16).reshape(span, feats)
     section_three = section_two + lay.own_sum(product(swish_low, narrow_own))
-    section_three, cotangent = lax.optimization_barrier((section_three, cotangent))
-    grad_entry = lay.enter(cotangent)
     branch_four, saved_four = feed_forward(
         section_three, gain_rows[3], shift_rows[3], up_two, down_two
     )
     section_four = section_three + 0.5 * branch_four
     final_out, final_normal, final_inv = norm_fwd(section_four, gain_rows[4], shift_rows[4])
-    output = lay.leave(final_out.astype(bf16).reshape(utt_count, block_len, D))
-
-    grad_final = grad_entry.astype(f32).reshape(rows, D)
+    final_low = final_out.astype(bf16).reshape(utt_count, block_len, D)
+
+    grad_final = lay.entered(entries).astype(f32).reshape(rows, D)
     grad_four, gain_four, shift_four = norm_back(grad_final, final_normal, final_inv, gain_rows[4])
 
     def scatter_two(grad_down, grad_up, grad_hidden):
-        moved = lay.scatter([grad_up, grad_down])
-        return grad_hidden, moved
-
-    grad_mid, moved_two, gain_three, shift_three = feed_back(
+        grad_up, grad_hidden = lax.optimization_barrier((grad_up, grad_hidden))
+        return grad_hidden, (lay.scatter([grad_up]), lay.scatter([grad_down]))
+
+    grad_mid, (moved_up_two, moved_down_two), gain_three, shift_three = feed_back(
         0.5 * grad_four, saved_four, gain_rows[3], up_two, down_two, scatter_two
     )
     grad_three = grad_four + grad_mid
@@ -697,7 +737,7 @@
         lay.own_sum(product_nt(grad_wide_out, wide_own)), conv_normal, conv_inv, gain_rows[2]
     )
     grad_two = grad_three + grad_conv_in
-    merge_low, output = lax.optimization_barrier((grad_two.astype(bf16), output))
+    merge_low = grad_two.astype(bf16)
     grad_merge = product_tn(attended_low, merge_low).astype(bf16)
     grad_merge = jnp.concatenate(
         [
@@ -715,12 +755,15 @@
         [grad_attended[:, 0]]
         + [lay.send(grad_attended[:, s], lay.to_class(s)) for s in range(1, size)]
     )
-    grad_attended, rows_two = lax.optimization_barrier((grad_attended, moved_two[0]))
-    moved_conv = lay.scatter([grad_merge, grad_wide.reshape(D, D), grad_narrow], after=rows_two)
+    grad_attended, final_low = lax.optimization_barrier((grad_attended, final_low))
+    output = lay.leave(final_low)
+    moved_conv = lay.scatter([grad_merge, grad_wide.reshape(D, D), grad_narrow])
     grad_query, grad_key, grad_value, grad_rel, grad_biases = attend_back(
         own_at, joint_out, rel_low, bias_rows, key_mask, attended, grad_attended, log_totals
     )
-    grad_query, rows_conv = lax.optimization_barrier((grad_query, moved_conv[0]))
+    grad_query, rows_up_two, rows_down_two, rows_conv, output = lax.optimization_barrier(
+        (grad_query, moved_up_two[0], moved_down_two[0], moved_conv[0], output)
+    )
     grad_biases = grad_biases.transpose(1, 0, 2).reshape(2, feats)
     rel_high = grad_rel.astype(bf16)
     rel_rest = (grad_rel - rel_high.astype(f32)).astype(bf16)
@@ -735,25 +778,30 @@
         lay.own_sum(product_nt(grad_joint_out, joint_own)), att_normal, att_inv, gain_rows[1]
     )
     grad_one = grad_two + grad_att_in
+    earlier = (rows_up_two, rows_down_two, rows_conv, output)
     moved_joint = lay.scatter(
-        [grad_joint.reshape(D, 3 * D // 2), grad_rel_proj], over_planes=True, after=rows_conv
+        [grad_joint.reshape(D, 3 * D // 2), grad_rel_proj], after=rows_conv
     )
 
     def scatter_one(grad_down, grad_up, grad_hidden):
         grad_hidden, rows_joint = lax.optimization_barrier((grad_hidden, moved_joint[0]))
         moved_down = lay.scatter([grad_down], after=rows_joint)
         moved_up = lay.scatter([grad_up], over_planes=True, after=moved_down[0])
-        return grad_hidden, (moved_down, moved_up)
-
-    grad_first, (moved_down, moved_up), gain_zero, shift_zero = feed_back(
+        late, _ = lax.optimization_barrier((earlier + (rows_joint,), grad_up))
+        return grad_hidden, (moved_down, moved_up, late)
+
+    grad_first, (moved_down, moved_up, late), gain_zero, shift_zero = feed_back(
         0.5 * grad_one, saved_one, gain_rows[0], up_one, down_one, scatter_one
     )
     grad_zero = grad_one + grad_first
-    grad_inputs = lay.leave(grad_zero.astype(bf16).reshape(utt_count, block_len, D))
-
-    summed_up_two, summed_down_two = lay.collect(rows_two, moved_two[1])
+    grad_inputs = lay.left(lay.leave(grad_zero.astype(bf16).reshape(utt_count, block_len, D)))
+
+    rows_up_two, rows_down_two, rows_conv, output, rows_joint = late
+    output = lay.left(output)
+    (summed_up_two,) = lay.collect(rows_up_two, moved_up_two[1])
+    (summed_down_two,) = lay.collect(rows_down_two, moved_down_two[1])
     summed_merge, summed_wide, summed_narrow = lay.collect(rows_conv, moved_conv[1])
-    summed_joint, summed_rel = lay.collect(*moved_joint)
+    summed_joint, summed_rel = lay.collect(rows_joint, moved_joint[1])
     (summed_down_one,) = lay.collect(*moved_down)
     (summed_up_one,) = lay.collect(*moved_up)
     summed_up_one = lay.cols_join(summed_up_one, tm)

time: 1370 us -> 1270 us (0.927)
  waiting for transfers between devices: 424 us -> 355 us
  other arithmetic: 197 us -> 181 us
  local copies, waits for them, and re-layouts: 168 us -> 154 us
    ppermute x8, waiting for transfers between devices: 81.3 us -> 34.7 us  [leave(): received.append(lax.ppermute(block, AXES, [(b, a) for a, b in there]))]
    all_gather x4 -> x2, waiting for transfers between devices: 104 us -> 67.1 us  [gather(): lax.all_gather(packed[None], AXES, axis=0, tiled=True, axis_index_groups=...]
    reduce_scatter x5 -> x6, waiting for transfers between devices: 37.5 us -> 73 us  [scatter(): lax.psum_scatter(mine, 'tm', scatter_dimension=0, tiled=True)]
    ppermute x57 -> x60, waiting for transfers between devices: 201 us -> 180 us  [send(): return lax.ppermute(values, AXES, self.route(target))]
    ppermute x57 -> x60, starting transfers between devices: 75.5 us -> 69.1 us  [send(): return lax.ppermute(values, AXES, self.route(target))]
    unnamed x350 -> x357, local copies, waits for them, and re-layouts: 49.8 us -> 44.6 us
    another operation x4 -> x3, other arithmetic: 43.2 us -> 41.5 us
  transfers between devices with their start and end apart: 74 -> 76, of which waited for: 35 -> 37; matrix products, arithmetic and copies ran while one was open for 35% -> 34% of each run, Pallas kernels for 14% -> 15%
where the time goes in v2:
time: 1270 us
  waiting for transfers between devices  355 us (28%)
  matrix products  267 us (21%)
  Pallas kernels  195 us (15%)
  other arithmetic  181 us (14%)
  local copies, waits for them, and re-layouts  154 us (12%)
  starting transfers between devices  94.7 us (7%)
  between operations  19 us (1%)
    ppermute x60, waiting for transfers between devices, send(): return lax.ppermute(values, AXES, self.route(target))  180 us
    pallas_call x1, Pallas kernels, attend_back(): pl.pallas_call(functools.partial(attend_back_kernel, slots=slots, rows=ro...  136 us
    dot_general x10, matrix products, product_tn(): lax.dot_general(left, right, (((0,), (0,)), ((), ())), preferred_element_...  93.5 us
    dot_general x9, matrix products, product(): return jnp.dot(left, right, preferred_element_type=f32)  88.4 us
    dot_general x8, matrix products, product_nt(): lax.dot_general(left, right, (((1,), (1,)), ((), ())), preferred_element_...  85.5 us
    reduce_scatter x6, waiting for transfers between devices, scatter(): lax.psum_scatter(mine, 'tm', scatter_dimension=0, tiled=True)  73 us
    ppermute x60, starting transfers between devices, send(): return lax.ppermute(values, AXES, self.route(target))  69.1 us
    all_gather x2, waiting for transfers between devices, gather(): lax.all_gather(packed[None], AXES, axis=0, tiled=True, axis_index_groups=...  67.1 us
  transfers between devices with their start and end apart: 76, of which 37 were waited for; matrix products, arithmetic and copies ran while one was open for 34% of the time, Pallas kernels for 15%

profile of v2, /device:TPU:11, one launch (start us, length us, event | category | flops | bytes accessed | tf_op | source)
XLA Modules:
  0.0 1267.0 jit_solution(6762262233772510810)
XLA Ops:
  44.2 32.8 %collective-permute-done.5 = bf16[2,19,128]{2,1,0:T(8,128)(2,1)S(1)} collective-permute-done((bf16[2,19,128]{2,1,0:T(8,128)(2,1)S(1)}, bf16[2,19,128]{2,1,0:T(8,128)(2,1)S(1)}, u32[]{:S(2)}, u32[]{:S(2)}) %collective-permute-start.5) | collective-permute-done | bytes 9760 | tf_op jit(solution)/shard_map/ppermute | solution.py:286
  79.7 26.9 %collective-permute-done.6 = bf16[4,19,128]{2,1,0:T(8,128)(2,1)S(1)} collective-permute-done((bf16[4,19,128]{2,1,0:T(8,128)(2,1)S(1)}, bf16[4,19,128]{2,1,0:T(8,128)(2,1)S(1)}, u32[]{:S(2)}, u32[]{:S(2)}) %collective-permute-start.6) | collective-permute-done | bytes 19488 | tf_op jit(solution)/shard_map/ppermute | solution.py:286
  115.4 32.8 %fusion = (bf16[4096,512]{1,0:T(8,128)(2,1)}, bf16[4096,512]{1,0:T(8,128)(2,1)}) fusion(f32[512]{0:T(512)S(1)} %multiply_exponential_fusion, f32[4096]{0:T(1024)S(1)} %subtract_convert_fusion.4), kind=kLoop, calls=%fused_computation.9 | loop fusion | flops 6291456 | bytes 8407040 | tf_op jit(solution)/shard_map/convert.39
  156.1 45.2 %all-gather.5.cloned.1.call-done = bf16[6144,1024]{1,0:T(8,128)(2,1)} async-done(((bf16[384,1024]{1,0:T(8,128)(2,1)}), bf16[6144,1024]{1,0:T(8,128)(2,1)}) %all-gather.5.cloned.1.call-update) | async-done | bytes 12582928 | tf_op jit(solution)/shard_map/all_gather | solution.py:419
  211.3 19.7 %multiply_convert_fusion.3 = (bf16[2048,2048]{1,0:T(8,128)(2,1)}, f32[2048,2048]{1,0:T(8,128)}) fusion(bf16[1024,2048]{1,0:T(8,128)(2,1)S(1)} %bitcast.401, bf16[1024,1024]{1,0:T(8,128)(2,1)} %collective-permute-done.7, bf16[1024,1024]{1,0:T(8,128)(2,1)} %fusion.35), kind=kOutput, calls=%fused_computation.5 | convolution fusion | flops 8619294720 | bytes 33554432 | tf_op jit(solution)/shard_map/dot_general | solution.py:25
  231.1 11.7 fusion.142
  282.6 58.5 %attend.1 = (bf16[2,1024,512]{2,1,0:T(8,128)(2,1)}, f32[4,2048,1]{2,1,0:T(8,128)}) custom-call(s32[1]{0:T(128)} %bitcast.own_ref, bf16[2,1024,1536]{2,1,0:T(8,128)(2,1)} %bitcast.516, bf16[2,1024,1536]{2,1,0:T(8,128)(2,1)} %bitcast.517, bf16[2,1024,1536]{2,1,0:T(8,128)(2,1)} %bitcast.518, bf16[4096,512]{1,0:T(8,128)(2,1)} %convolution_convert_fusion.1.rel_ref, ...), custom_call_target="tpu_custom_call" | custom-call | flops 42949672960 | bytes 20971520 | tf_op jit(solution)/shard_map/attend/pallas_call | solution.py:174
  342.9 22.0 %all-gather.7.cloned.1.call-done = bf16[6656,1024]{1,0:T(8,128)(2,1)} async-done(((bf16[416,1024]{1,0:T(8,128)(2,1)}), bf16[6656,1024]{1,0:T(8,128)(2,1)}) %all-gather.7.cloned.1.call-update) | async-done | bytes 13631504 | tf_op jit(solution)/shard_map/all_gather | solution.py:419
  423.0 13.2 %collective-permute-done.14 = bf16[1,256,1024]{2,1,0:T(8,128)(2,1)S(1)} collective-permute-done((bf16[1,256,1024]{2,1,0:T(8,128)(2,1)S(1)}, bf16[1,256,1024]{2,1,0:T(8,128)(2,1)S(1)}, u32[]{:S(2)}, u32[]{:S(2)}) %collective-permute-start.14) | collective-permute-done | bytes 524320 | tf_op jit(solution)/shard_map/ppermute | solution.py:286
  470.5 18.7 %multiply_convert_fusion.2 = (bf16[2048,2048]{1,0:T(8,128)(2,1)}, f32[2048,2048]{1,0:T(8,128)}) fusion(bf16[1024,2048]{1,0:T(8,128)(2,1)S(1)} %bitcast.407, bf16[1024,1024]{1,0:T(8,128)(2,1)} %copy-done.146, bf16[1024,1024]{1,0:T(8,128)(2,1)S(1)} %add_convert_fusion.2), kind=kOutput, calls=%fused_computation.3 | convolution fusion | flops 8619294720 | bytes 33554432 | tf_op jit(solution)/shard_map/dot_general | solution.py:25
  529.5 20.6 %multiply_convert_fusion.1 = bf16[2048,2048]{1,0:T(8,128)(2,1)} fusion(f32[2048,2048]{1,0:T(8,128)} %get-tuple-element.352, bf16[2048,1024]{1,0:T(8,128)(2,1)} %pad_maximum_fusion.11, bf16[2048,1024]{1,0:T(8,128)(2,1)} %bitcast.410), kind=kOutput, calls=%fused_computation.2 | convolution fusion | flops 8627683328 | bytes 33554432 | tf_op jit(solution)/shard_map/dot_general | solution.py:29
  550.1 14.7 %convolution_convert_fusion.4 = bf16[1024,2048]{1,0:T(8,128)(2,1)} fusion(bf16[2048,2048]{1,0:T(8,128)(2,1)} %multiply_convert_fusion.1, bf16[1024,1024]{1,0:T(8,128)(2,1)} %copy-done.146, bf16[1024,1024]{1,0:T(8,128)(2,1)} %copy-done.47), kind=kOutput, calls=%fused_computation.146 | convolution fusion | flops 8600420352 | bytes 16777216 | tf_op jit(solution)/shard_map/dot_general | solution.py:33
  564.8 11.5 fusion.146
  723.2 136.5 %attend_back.1 = (bf16[2,1024,512]{2,1,0:T(8,128)(2,1)}, bf16[2,1024,512]{2,1,0:T(8,128)(2,1)}, bf16[2,1024,512]{2,1,0:T(8,128)(2,1)}, f32[4096,512]{1,0:T(8,128)}, f32[4,2,128]{2,1,0:T(2,128)}) custom-call(s32[1]{0:T(128)} %bitcast.own_ref, bf16[2,1024,1536]{2,1,0:T(8,128)(2,1)} %bitcast.519, bf16[2,1024,1536]{2,1,0:T(8,128)(2,1)} %bitcast.520, ...), custom_call_target="tpu_custom_call" | custom-call | flops 107374182400 | bytes 41943040 | tf_op jit(solution)/shard_map/attend_back/pallas_call | solution.py:204
  859.8 45.9 %reduce-scatter.11.cloned.1.call-done = bf16[1,2,160,1024]{3,2,1,0:T(8,128)(2,1)} async-done(((bf16[8,2,160,1024]{3,2,1,0:T(8,128)(2,1)}), bf16[1,2,160,1024]{3,2,1,0:T(8,128)(2,1)}) %reduce-scatter.11.cloned.1.call-update) | async-done | bytes 655376 | tf_op jit(solution)/shard_map/reduce_scatter | solution.py:438
  926.4 11.3 add_convert_fusion.5
  956.3 13.8 %convolution_convert_fusion.5 = bf16[2048,1024]{1,0:T(8,128)(2,1)} fusion(bf16[2048,2048]{1,0:T(8,128)(2,1)} %get-tuple-element.347, bf16[1024,1024]{1,0:T(8,128)(2,1)} %collective-permute-done.39, bf16[1024,1024]{1,0:T(8,128)(2,1)S(1)} %get-tuple-element.186), kind=kOutput, calls=%fused_computation.147 | convolution fusion | flops 8600420352 | bytes 16777216 | tf_op jit(solution)/shard_map/dot_general | solution.py:33
  974.4 20.0 %multiply_convert_fusion = bf16[2048,2048]{1,0:T(8,128)(2,1)} fusion(f32[2048,2048]{1,0:T(8,128)} %get-tuple-element.348, bf16[2048,1024]{1,0:T(8,128)(2,1)} %pad_maximum_fusion.16, bf16[2048,1024]{1,0:T(8,128)(2,1)S(1)} %bitcast.404), kind=kOutput, calls=%fused_computation.1 | convolution fusion | flops 8627683328 | bytes 33554432 | tf_op jit(solution)/shard_map/dot_general | solution.py:29
  994.4 13.0 %convolution_convert_fusion.3 = bf16[1024,2048]{1,0:T(8,128)(2,1)S(1)} fusion(bf16[2048,2048]{1,0:T(8,128)(2,1)} %multiply_convert_fusion, bf16[1024,1024]{1,0:T(8,128)(2,1)} %collective-permute-done.7, bf16[1024,1024]{1,0:T(8,128)(2,1)} %fusion.35), kind=kOutput, calls=%fused_computation.145 | convolution fusion | flops 8600420352 | bytes 16777216 | tf_op jit(solution)/shard_map/dot_general | solution.py:33
  1018.2 25.6 %reduce-scatter.13.cloned.1.call-done = bf16[1,2,128,1024]{3,2,1,0:T(8,128)(2,1)} async-done(((bf16[8,2,128,1024]{3,2,1,0:T(8,128)(2,1)}), bf16[1,2,128,1024]{3,2,1,0:T(8,128)(2,1)}) %reduce-scatter.13.cloned.1.call-update) | async-done | bytes 524304 | tf_op jit(solution)/shard_map/reduce_scatter | solution.py:438
  1044.3 12.4 collective-permute-done.45
  1060.7 12.8 %fusion.148 = f32[2048,1024]{1,0:T(8,128)S(1)} fusion(bf16[2048,2048]{1,0:T(8,128)(2,1)} %multiply_convert_fusion, bf16[1024,2048]{1,0:T(8,128)(2,1)} %bitcast.402), kind=kOutput, calls=%fused_computation.495 | convolution fusion | flops 8589934592 | bytes 20971520 | tf_op jit(solution)/shard_map/dot_general | solution.py:29
  1209.4 11.7 collective-permute-done.42
  1223.8 14.3 %collective-permute-done.43 = bf16[1,256,1024]{2,1,0:T(8,128)(2,1)} collective-permute-done((bf16[1,256,1024]{2,1,0:T(8,128)(2,1)}, bf16[1,256,1024]{2,1,0:T(8,128)(2,1)}, u32[]{:S(2)}, u32[]{:S(2)}) %collective-permute-start.43) | collective-permute-done | bytes 524320 | tf_op jit(solution)/shard_map/ppermute | solution.py:326
  (832 shorter events, 602.3 us)
Async XLA Ops:
  7.2 194.1 %all-gather.5.cloned.1.call-start = ((), (), s32[]{:S(2)}) async-start(), calls=%async_computation.12 | async-start | bytes 13369344 | tf_op jit(solution)/shard_map/all_gather | solution.py:419
  14.0 350.9 %all-gather.7.cloned.1.call-start = ((), (), s32[]{:S(2)}) async-start(), calls=%async_computation.13 | async-start | bytes 14483456 | tf_op jit(solution)/shard_map/all_gather | solution.py:419
  22.6 837.2 %reduce-scatter.7.cloned.1.call-start = ((), (), s32[]{:S(2)}) async-start(), calls=%async_computation.6 | async-start | bytes 4718592 | tf_op jit(solution)/shard_map/reduce_scatter | solution.py:438
  23.9 84.6 %collective-permute-start = (bf16[1,256,1024]{2,1,0:T(8,128)(2,1)S(1)}, bf16[1,256,1024]{2,1,0:T(8,128)(2,1)}, u32[]{:S(2)}, u32[]{:S(2)}) collective-permute-start(bf16[1,256,1024]{2,1,0:T(8,128)(2,1)S(1)} %get-tuple-element.274), channel_id=1, source_target_pairs={{0,0},{1,2},{2,4},{3,6},{4,8},{5,10},{6,12},{7,14},{8,1},{9,3},{10... | collective-permute-start | bytes 1572872 | tf_op jit(solution)/shard_map/ppermute | solution.py:286
  28.7 81.3 %collective-permute-start.1 = (bf16[1,256,1024]{2,1,0:T(8,128)(2,1)}, bf16[1,256,1024]{2,1,0:T(8,128)(2,1)}, u32[]{:S(2)}, u32[]{:S(2)}) collective-permute-start(bf16[1,256,1024]{2,1,0:T(8,128)(2,1)} %get-tuple-element.273), channel_id=1, source_target_pairs={{0,2},{1,4},{2,6},{3,0},{4,10},{5,12},{6,14},{7,8},{8,3},{9,5},{10... | collective-permute-start | bytes 1572872 | tf_op jit(solution)/shard_map/ppermute | solution.py:286
  30.6 80.5 %collective-permute-start.2 = (bf16[1,256,1024]{2,1,0:T(8,128)(2,1)}, bf16[1,256,1024]{2,1,0:T(8,128)(2,1)S(1)}, u32[]{:S(2)}, u32[]{:S(2)}) collective-permute-start(bf16[1,256,1024]{2,1,0:T(8,128)(2,1)} %get-tuple-element.272), channel_id=1, source_target_pairs={{0,4},{1,6},{2,0},{3,2},{4,12},{5,14},{6,8},{7,10},{8,5},{9,7},{10... | collective-permute-start | bytes 1572872 | tf_op jit(solution)/shard_map/ppermute | solution.py:286
  31.0 80.1 %collective-permute-start.3 = (bf16[1,256,1024]{2,1,0:T(8,128)(2,1)}, bf16[1,256,1024]{2,1,0:T(8,128)(2,1)S(1)}, u32[]{:S(2)}, u32[]{:S(2)}) collective-permute-start(bf16[1,256,1024]{2,1,0:T(8,128)(2,1)} %get-tuple-element.271), channel_id=1, source_target_pairs={{0,6},{1,0},{2,2},{3,4},{4,14},{5,8},{6,10},{7,12},{8,7},{9,1},{10... | collective-permute-start | bytes 1572872 | tf_op jit(solution)/shard_map/ppermute | solution.py:286
  114.5 96.8 %collective-permute-start.7 = (bf16[1024,1024]{1,0:T(8,128)(2,1)}, bf16[1024,1024]{1,0:T(8,128)(2,1)}, u32[]{:S(2)}, u32[]{:S(2)}) collective-permute-start(bf16[1024,1024]{1,0:T(8,128)(2,1)} %fusion.35), channel_id=1, source_target_pairs={{0,8},{1,9},{2,10},{3,11},{4,12},{5,13},{6,14},{7,15},{8,0},{9,1},... | collective-permute-start | bytes 6291464 | tf_op jit(solution)/shard_map/ppermute | solution.py:286
  388.5 47.7 %collective-permute-start.14 = (bf16[1,256,1024]{2,1,0:T(8,128)(2,1)S(1)}, bf16[1,256,1024]{2,1,0:T(8,128)(2,1)S(1)}, u32[]{:S(2)}, u32[]{:S(2)}) collective-permute-start(bf16[1,256,1024]{2,1,0:T(8,128)(2,1)S(1)} %get-tuple-element.265), channel_id=1, source_target_pairs={{0,2},{1,4},{2,6},{3,0},{4,10},{5,12},{6,14},{7,8},{8,3},{9,5},{10... | collective-permute-start | bytes 1572872 | tf_op jit(solution)/shard_map/ppermute | solution.py:286
  390.4 45.8 %collective-permute-start.15 = (bf16[1,256,1024]{2,1,0:T(8,128)(2,1)S(1)}, bf16[1,256,1024]{2,1,0:T(8,128)(2,1)}, u32[]{:S(2)}, u32[]{:S(2)}) collective-permute-start(bf16[1,256,1024]{2,1,0:T(8,128)(2,1)S(1)} %get-tuple-element.264), channel_id=1, source_target_pairs={{0,4},{1,6},{2,0},{3,2},{4,12},{5,14},{6,8},{7,10},{8,5},{9,7},{10... | collective-permute-start | bytes 1572872 | tf_op jit(solution)/shard_map/ppermute | solution.py:286
  390.9 45.4 %collective-permute-start.16 = (bf16[1,256,1024]{2,1,0:T(8,128)(2,1)S(1)}, bf16[1,256,1024]{2,1,0:T(8,128)(2,1)}, u32[]{:S(2)}, u32[]{:S(2)}) collective-permute-start(bf16[1,256,1024]{2,1,0:T(8,128)(2,1)S(1)} %get-tuple-element.263), channel_id=1, source_target_pairs={{0,6},{1,0},{2,2},{3,4},{4,14},{5,8},{6,10},{7,12},{8,7},{9,1},{10... | collective-permute-start | bytes 1572872 | tf_op jit(solution)/shard_map/ppermute | solution.py:286
  595.2 264.6 %reduce-scatter.9.cloned.1.call-start = ((), (), s32[]{:S(2)}) async-start(), calls=%async_computation.7 | async-start | bytes 4718592 | tf_op jit(solution)/shard_map/reduce_scatter | solution.py:438
  651.0 254.7 %reduce-scatter.11.cloned.1.call-start = ((), (), s32[]{:S(2)}) async-start(), calls=%async_computation.8 | async-start | bytes 5898240 | tf_op jit(solution)/shard_map/reduce_scatter | solution.py:438
  705.0 338.9 %reduce-scatter.13.cloned.1.call-start = ((), (), s32[]{:S(2)}) async-start(), calls=%async_computation.9 | async-start | bytes 4718592 | tf_op jit(solution)/shard_map/reduce_scatter | solution.py:438
  710.8 149.0 %collective-permute-start.34 = (bf16[1,256,1024]{2,1,0:T(8,128)(2,1)S(1)}, bf16[1,256,1024]{2,1,0:T(8,128)(2,1)}, u32[]{:S(2)}, u32[]{:S(2)}) collective-permute-start(bf16[1,256,1024]{2,1,0:T(8,128)(2,1)S(1)} %get-tuple-element.250), channel_id=1, source_target_pairs={{0,0},{2,1},{4,2},{6,3},{8,4},{10,5},{12,6},{14,7},{1,8},{3,9},{5,... | collective-permute-start | bytes 1572872 | tf_op jit(solution)/shard_map/ppermute | solution.py:326
  713.6 146.1 %collective-permute-start.35 = (bf16[1,256,1024]{2,1,0:T(8,128)(2,1)S(1)}, bf16[1,256,1024]{2,1,0:T(8,128)(2,1)}, u32[]{:S(2)}, u32[]{:S(2)}) collective-permute-start(bf16[1,256,1024]{2,1,0:T(8,128)(2,1)S(1)} %get-tuple-element.249), channel_id=1, source_target_pairs={{2,0},{4,1},{6,2},{0,3},{10,4},{12,5},{14,6},{8,7},{3,8},{5,9},{7,... | collective-permute-start | bytes 1572872 | tf_op jit(solution)/shard_map/ppermute | solution.py:326
  718.4 141.3 %collective-permute-start.36 = (bf16[1,256,1024]{2,1,0:T(8,128)(2,1)S(1)}, bf16[1,256,1024]{2,1,0:T(8,128)(2,1)}, u32[]{:S(2)}, u32[]{:S(2)}) collective-permute-start(bf16[1,256,1024]{2,1,0:T(8,128)(2,1)S(1)} %get-tuple-element.248), channel_id=1, source_target_pairs={{4,0},{6,1},{0,2},{2,3},{12,4},{14,5},{8,6},{10,7},{5,8},{7,9},{1,... | collective-permute-start | bytes 1572872 | tf_op jit(solution)/shard_map/ppermute | solution.py:326
  719.2 140.6 %collective-permute-start.37 = (bf16[1,256,1024]{2,1,0:T(8,128)(2,1)S(1)}, bf16[1,256,1024]{2,1,0:T(8,128)(2,1)}, u32[]{:S(2)}, u32[]{:S(2)}) collective-permute-start(bf16[1,256,1024]{2,1,0:T(8,128)(2,1)S(1)} %get-tuple-element.247), channel_id=1, source_target_pairs={{6,0},{0,1},{2,2},{4,3},{14,4},{8,5},{10,6},{12,7},{7,8},{1,9},{3,... | collective-permute-start | bytes 1572872 | tf_op jit(solution)/shard_map/ppermute | solution.py:326
  956.3 193.0 %reduce-scatter.15.cloned.1.call-start = ((), (), s32[]{:S(2)}) async-start(), calls=%async_computation.10 | async-start | bytes 4718592 | tf_op jit(solution)/shard_map/reduce_scatter | solution.py:438
  1009.6 47.1 %collective-permute-start.45 = (bf16[8,128,1024]{2,1,0:T(8,128)(2,1)}, bf16[8,128,1024]{2,1,0:T(8,128)(2,1)}, u32[]{:S(2)}, u32[]{:S(2)}) collective-permute-start(bf16[8,128,1024]{2,1,0:T(8,128)(2,1)} %pad_maximum_fusion.32), channel_id=1, source_target_pairs={{0,16},{1,17},{2,18},{3,19},{4,20},{5,21},{6,22},{7,23},{8,24},{9,... | collective-permute-start | bytes 6291464 | tf_op jit(solution)/shard_map/ppermute | solution.py:286
  1043.9 178.7 %reduce-scatter.17.cloned.1.call-start = ((), (), s32[]{:S(2)}) async-start(), calls=%async_computation.11 | async-start | bytes 2359296 | tf_op jit(solution)/shard_map/reduce_scatter | solution.py:438
  1075.2 77.9 %collective-permute-start.40 = (bf16[1024,1024]{1,0:T(8,128)(2,1)}, bf16[1024,1024]{1,0:T(8,128)(2,1)}, u32[]{:S(2)}, u32[]{:S(2)}) collective-permute-start(bf16[1024,1024]{1,0:T(8,128)(2,1)} %slice.831), channel_id=1, source_target_pairs={{0,8},{1,9},{2,10},{3,11},{4,12},{5,13},{6,14},{7,15},{8,0},{9,1},... | collective-permute-start | bytes 6291464 | tf_op jit(solution)/shard_map/ppermute | solution.py:286
  1197.2 50.6 %collective-permute-start.44 = (bf16[1,256,1024]{2,1,0:T(8,128)(2,1)}, bf16[1,256,1024]{2,1,0:T(8,128)(2,1)}, u32[]{:S(2)}, u32[]{:S(2)}) collective-permute-start(bf16[1,256,1024]{2,1,0:T(8,128)(2,1)} %get-tuple-element.243), channel_id=1, source_target_pairs={{6,0},{0,1},{2,2},{4,3},{14,4},{8,5},{10,6},{12,7},{7,8},{1,9},{3,... | collective-permute-start | bytes 1572872 | tf_op jit(solution)/shard_map/ppermute | solution.py:326
  1207.4 44.8 %collective-permute-start.50 = (bf16[2,128,1024]{2,1,0:T(8,128)(2,1)S(1)}, bf16[2,128,1024]{2,1,0:T(8,128)(2,1)S(1)}, u32[]{:S(2)}, u32[]{:S(2)}) collective-permute-start(bf16[2,128,1024]{2,1,0:T(8,128)(2,1)S(1)} %constant_dynamic-update-slice_fusion.21), channel_id=1, source_target_pairs={{0,8},{1,9},{2,10},{3,11},{4,12},{5,13},{6,14},{7,15},{8,0},{9,1},... | collective-permute-start | bytes 1572872 | tf_op jit(solution)/shard_map/ppermute | solution.py:286
  (215 other events, 2342.9 us)
Sparse Core Ops, SparseCore 0:
  14.1 187.0 all-gather.4
  204.7 160.1 all-gather.6
  595.3 89.4 reduce-scatter.6
  688.7 111.3 reduce-scatter.8
  803.5 102.1 reduce-scatter.10
  956.4 87.4 reduce-scatter.12
  1047.9 87.8 reduce-scatter.14
  1149.4 73.2 reduce-scatter.16

commit v3 on v2

--- a/solution.py
+++ b/solution.py
@@ -46,11 +46,30 @@
     return query_u, query_v
 
 
-def slot_scores(query_u, query_v, key, rel_window, mask_row, rows, tile):
+def shifted_rel(query_v, rel_window, rows, tile):
     width = rows + tile
     raw = product_nt(query_v, rel_window)
-    shifted = pltpu.roll(raw, width - (tile - 1), 1, stride=1, stride_axis=0)[:, :rows]
-    return shifted + product_nt(query_u, key) + mask_row
+    return pltpu.roll(raw, width - (tile - 1), 1, stride=1, stride_axis=0)[:, :rows]
+
+
+def three_parts(column):
+    high = column.astype(bf16).astype(f32)
+    middle = (column - high).astype(bf16).astype(f32)
+    return high, middle, column - high - middle
+
+
+def widened(values, mask_factor, column=None):
+    lane = lax.broadcasted_iota(jnp.int32, (values.shape[0], HEAD_DIM), 1)
+    extra = jnp.where(lane == 0, mask_factor, 0.0)
+    if column is not None:
+        for at, part in enumerate(three_parts(column)):
+            extra = jnp.where(lane == at + 1, part, extra)
+    return jnp.concatenate([values, extra.astype(bf16)], axis=1)
+
+
+def fill_wide(wide_ref, ref, extra_ref):
+    wide_ref[:, :, :HEAD_DIM] = ref[...]
+    wide_ref[:, :, HEAD_DIM:] = extra_ref[...]
 
 
 def attend_kernel(
@@ -63,10 +82,9 @@
     top = jnp.full((tile, 1), -jnp.inf, f32)
     for s in range(slots):
         base = pl.multiple_of(slots * rows - tile - start + (own ^ s) * rows, tile)
-        scores = slot_scores(
-            query_u, query_v, k_ref[s], rel_ref[pl.ds(base, rows + tile), :],
-            mask_ref[0:1, s * rows : (s + 1) * rows], rows, tile,
-        )
+        scores = shifted_rel(query_v, rel_ref[pl.ds(base, rows + tile), :], rows, tile)
+        scores = scores + product_nt(query_u, k_ref[s])
+        scores = scores + mask_ref[0:1, s * rows : (s + 1) * rows]
         score_ref[s] = scores
         top = jnp.maximum(top, jnp.max(scores, axis=1, keepdims=True))
     total = jnp.zeros((tile, 1), f32)
@@ -80,8 +98,9 @@
 
 
 def attend_back_kernel(
-    own_ref, q_ref, k_ref, v_ref, rel_ref, bias_ref, mask_ref, o_ref, do_ref, lse_ref,
-    dq_ref, dk_ref, dv_ref, drel_ref, dbias_ref, dk_acc, dv_acc, *, slots, rows, tile
+    own_ref, q_ref, k_ref, v_ref, rel_ref, bias_ref, extra_ref, o_ref, do_ref, lse_ref,
+    dq_ref, dk_ref, dv_ref, drel_ref, dbias_ref, dk_acc, dv_acc, key_ref, value_ref,
+    *, slots, rows, tile
 ):
     own = own_ref[0]
     tile_at = pl.program_id(1)
@@ -90,6 +109,8 @@
 
     @pl.when(tile_at == 0)
     def _():
+        fill_wide(key_ref, k_ref, extra_ref)
+        fill_wide(value_ref, v_ref, extra_ref)
         dk_acc[...] = jnp.zeros_like(dk_acc)
         dv_acc[...] = jnp.zeros_like(dv_acc)
         drel_ref[...] = jnp.zeros_like(drel_ref)
@@ -98,7 +119,8 @@
     query_u, query_v = biased_queries(q_ref, bias_ref)
     grad_out = do_ref[0]
     inner = jnp.sum(grad_out.astype(f32) * o_ref[0].astype(f32), axis=1, keepdims=True)
-    lse = lse_ref[0]
+    query_wide = widened(query_u, 1.0, -lse_ref[0])
+    grad_wide = widened(grad_out, 0.0, -inner)
     width = rows + tile
     row_at = lax.broadcasted_iota(jnp.int32, (tile, tile), 0)
     col_at = lax.broadcasted_iota(jnp.int32, (tile, tile), 1)
@@ -109,16 +131,12 @@
     for s in range(slots):
         base = pl.multiple_of(slots * rows - tile - start + (own ^ s) * rows, tile)
         rel_window = rel_ref[pl.ds(base, width), :]
-        key = k_ref[s]
-        scores = slot_scores(
-            query_u, query_v, key, rel_window, mask_ref[0:1, s * rows : (s + 1) * rows], rows, tile
-        )
-        probs = jnp.exp2(scores - lse)
-        grad_probs = product_nt(grad_out, v_ref[s])
-        grad_scores = (probs * (grad_probs - inner)).astype(bf16)
+        scores = shifted_rel(query_v, rel_window, rows, tile)
+        probs = jnp.exp2(scores + product_nt(query_wide, key_ref[s]))
+        grad_scores = (probs * product_nt(grad_wide, value_ref[s])).astype(bf16)
         dv_acc[s] += product_tn(probs.astype(bf16), grad_out)
         dk_acc[s] += product_tn(grad_scores, query_u)
-        grad_u = grad_u + product(grad_scores, key)
+        grad_u = grad_u + product(grad_scores, k_ref[s])
         flipped = product(flip, grad_scores).astype(bf16)
         padded = jnp.concatenate([flipped, jnp.zeros((tile, width - rows), bf16)], axis=1)
         grad_raw = pltpu.roll(padded, 0, 1, stride=1, stride_axis=0)
@@ -138,68 +156,54 @@
         drel_ref[...] = drel_ref[...] * (1.0 / LOG2E)
 
 
-def attention_specs(slots, rows, heads, tile, first):
+def attention_specs(slots, rows, heads, tile):
     per = rows // tile
     span = slots * rows
-    by_tile = pl.BlockSpec((1, tile, HEAD_DIM), lambda h, i, own: (i // per, i % per, first + h))
+    by_tile = pl.BlockSpec((1, tile, HEAD_DIM), lambda h, i, own: (i // per, i % per, h))
     in_specs = [
         by_tile,
-        pl.BlockSpec((slots, rows, HEAD_DIM), lambda h, i, own: (0, 0, heads + first + h)),
-        pl.BlockSpec((slots, rows, HEAD_DIM), lambda h, i, own: (0, 0, 2 * heads + first + h)),
-        pl.BlockSpec((2 * span, HEAD_DIM), lambda h, i, own: (0, first + h)),
-        pl.BlockSpec((2, HEAD_DIM), lambda h, i, own: (0, first + h)),
-        pl.BlockSpec((1, span), lambda h, i, own: (0, 0)),
+        pl.BlockSpec((slots, rows, HEAD_DIM), lambda h, i, own: (0, 0, heads + h)),
+        pl.BlockSpec((slots, rows, HEAD_DIM), lambda h, i, own: (0, 0, 2 * heads + h)),
+        pl.BlockSpec((2 * span, HEAD_DIM), lambda h, i, own: (0, h)),
+        pl.BlockSpec((2, HEAD_DIM), lambda h, i, own: (0, h)),
+        pl.BlockSpec((slots, rows, HEAD_DIM), lambda h, i, own: (0, 0, 0)),
     ]
     return slots * per, by_tile, in_specs
 
 
-def attend(own, joint, rel, bias, mask, first, count, before=None):
+def attend(own, joint, rel, bias, mask):
     slots, rows, wide = joint.shape
     heads = wide // (3 * HEAD_DIM)
     span, tile = slots * rows, min(256, rows)
-    tiles, by_tile, in_specs = attention_specs(slots, rows, heads, tile, first)
-    by_row = pl.BlockSpec((1, tile, 1), lambda h, i, own: (first + h, i, 0))
-    kernel = functools.partial(attend_kernel, slots=slots, rows=rows, tile=tile)
-    operands, aliases = (own, joint, joint, joint, rel, bias, mask), {}
-    if before is not None:
-        operands += tuple(before)
-        in_specs = in_specs + [pl.BlockSpec(memory_space=pl.ANY)] * 2
-        aliases = {7: 0, 8: 1}
-
-        def body_kernel(*refs):
-            kernel(*refs[:7], *refs[9:])
-
-    else:
-        body_kernel = kernel
+    tiles, by_tile, in_specs = attention_specs(slots, rows, heads, tile)
     return pl.pallas_call(
-        body_kernel,
+        functools.partial(attend_kernel, slots=slots, rows=rows, tile=tile),
         grid_spec=pltpu.PrefetchScalarGridSpec(
             num_scalar_prefetch=1,
-            grid=(count, tiles),
-            in_specs=in_specs,
-            out_specs=[by_tile, by_row],
+            grid=(heads, tiles),
+            in_specs=in_specs[:-1] + [pl.BlockSpec((1, span), lambda h, i, own: (0, 0))],
+            out_specs=[by_tile, pl.BlockSpec((1, tile, 1), lambda h, i, own: (h, i, 0))],
             scratch_shapes=[pltpu.VMEM((slots, tile, rows), f32)],
         ),
         out_shape=[
             jax.ShapeDtypeStruct((slots, rows, heads * HEAD_DIM), bf16),
             jax.ShapeDtypeStruct((heads, span, 1), f32),
         ],
-        input_output_aliases=aliases,
         compiler_params=pltpu.CompilerParams(vmem_limit_bytes=56 << 20),
         cost_estimate=pl.CostEstimate(
-            flops=count * span * span * HEAD_DIM * 20,
-            bytes_accessed=count * span * HEAD_DIM * 20,
-            transcendentals=count * span * span,
+            flops=heads * span * span * HEAD_DIM * 20,
+            bytes_accessed=heads * span * HEAD_DIM * 20,
+            transcendentals=heads * span * span,
         ),
         name="attend",
-    )(*operands)
-
-
-def attend_back(own, joint, rel, bias, mask, out, grad_out, lse):
+    )(own, joint, joint, joint, rel, bias, mask)
+
+
+def attend_back(own, joint, rel, bias, extra, out, grad_out, lse):
     slots, rows, wide = joint.shape
     heads = wide // (3 * HEAD_DIM)
     span, tile = slots * rows, min(256, rows)
-    tiles, by_tile, in_specs = attention_specs(slots, rows, heads, tile, 0)
+    tiles, by_tile, in_specs = attention_specs(slots, rows, heads, tile)
     by_head = pl.BlockSpec((slots, rows, HEAD_DIM), lambda h, i, own: (0, 0, h))
     return pl.pallas_call(
         functools.partial(attend_back_kernel, slots=slots, rows=rows, tile=tile),
@@ -215,7 +219,8 @@
                 pl.BlockSpec((2 * span, HEAD_DIM), lambda h, i, own: (0, h)),
                 pl.BlockSpec((1, 2, HEAD_DIM), lambda h, i, own: (h, 0, 0)),
             ],
-            scratch_shapes=[pltpu.VMEM((slots, rows, HEAD_DIM), f32)] * 2,
+            scratch_shapes=[pltpu.VMEM((slots, rows, HEAD_DIM), f32)] * 2
+            + [pltpu.VMEM((slots, rows, 2 * HEAD_DIM), bf16)] * 2,
         ),
         out_shape=[jax.ShapeDtypeStruct((slots, rows, heads * HEAD_DIM), bf16)] * 3
         + [
@@ -229,7 +234,7 @@
             transcendentals=heads * span * span,
         ),
         name="attend_back",
-    )(own, joint, joint, joint, rel, bias, mask, out, grad_out, lse)
+    )(own, joint, joint, joint, rel, bias, extra, out, grad_out, lse)
 
 
 def norm_fwd(values, gain_row, shift_row):
@@ -419,7 +424,7 @@
         full = lax.all_gather(packed[None], AXES, axis=0, tiled=True, axis_index_groups=groups)
         return [v.reshape(-1, v.shape[-1]) for v in unpack(full, places)]
 
-    def scatter(self, grads, over_planes=False, after=None):
+    def scatter(self, grads, over_planes=False, after=None, hold=None):
         plane = lax.axis_index("dp") // 2
         split = [g.astype(bf16).reshape(self.tm, self.pairs, -1, g.shape[-1]) for g in grads]
 
@@ -433,9 +438,12 @@
                 mine = (mine.astype(f32) + other.astype(f32)).astype(bf16)
         else:
             mine = jnp.stack([part(plane ^ s)[0] for s in range(self.pairs)], axis=1)
+        if hold is not None:
+            mine, hold = lax.optimization_barrier((mine, hold))
         if after is not None:
             mine, _ = lax.optimization_barrier((mine, after))
-        return lax.psum_scatter(mine, "tm", scatter_dimension=0, tiled=True), places
+        mine = lax.psum_scatter(mine, "tm", scatter_dimension=0, tiled=True)
+        return (mine, places) if hold is None else (mine, places, hold)
 
     def collect(self, mine, places):
         plane = lax.axis_index("dp") // 2
@@ -612,7 +620,10 @@
     frame_pos = slot_class[:, None] * rows + jnp.arange(rows, dtype=jnp.int32)[None, :]
     live = frame_pos < length
     live_col = live.astype(f32)[:, :, None]
-    key_mask = jnp.where(live, 0.0, neg_fill).astype(f32).reshape(1, span)
+    key_mask = jnp.where(live, 0.0, neg_fill).astype(f32)
+    key_extra = jnp.where(
+        jnp.arange(HEAD_DIM) == 0, key_mask[:, :, None], 1.0
+    ).astype(bf16)
     own_at = own.reshape(1).astype(jnp.int32)
 
     def framed_rows(values):
@@ -643,8 +654,9 @@
     att_low = lay.all_slots(att_normed.astype(bf16))
     joint_out = product(att_low, joint_own).astype(bf16).reshape(size, rows, 3 * feats)
     rel_low = product(table_low, rel_own).astype(bf16)
-    heads = feats // HEAD_DIM
-    attended, log_totals = attend(own_at, joint_out, rel_low, bias_rows, key_mask, 0, heads)
+    attended, log_totals = attend(
+        own_at, joint_out, rel_low, bias_rows, key_mask.reshape(1, span)
+    )
 
     merge_full, cotangent = lax.optimization_barrier((merge_full, cotangent))
     entries = [lay.enter(cotangent, k) for k in steps]
@@ -759,34 +771,34 @@
     output = lay.leave(final_low)
     moved_conv = lay.scatter([grad_merge, grad_wide.reshape(D, D), grad_narrow])
     grad_query, grad_key, grad_value, grad_rel, grad_biases = attend_back(
-        own_at, joint_out, rel_low, bias_rows, key_mask, attended, grad_attended, log_totals
+        own_at, joint_out, rel_low, bias_rows, key_extra, attended, grad_attended, log_totals
     )
     grad_query, rows_up_two, rows_down_two, rows_conv, output = lax.optimization_barrier(
         (grad_query, moved_up_two[0], moved_down_two[0], moved_conv[0], output)
     )
     grad_biases = grad_biases.transpose(1, 0, 2).reshape(2, feats)
+    grad_joint_out = jnp.concatenate([grad_query, grad_key, grad_value], axis=2).reshape(
+        span, 3 * feats
+    )
+    grad_joint = lay.sub_place(product_tn(att_low, grad_joint_out).reshape(D, 3, feats), 2)
+    *moved_joint, grad_joint_out = lay.scatter(
+        [grad_joint.reshape(D, 3 * D // 2)], hold=grad_joint_out
+    )
     rel_high = grad_rel.astype(bf16)
     rel_rest = (grad_rel - rel_high.astype(f32)).astype(bf16)
     grad_rel_proj = lay.sub_place(
         product_tn(table_low, rel_high) + product_tn(table_low, rel_rest), 1
     )
-    grad_joint_out = jnp.concatenate([grad_query, grad_key, grad_value], axis=2).reshape(
-        span, 3 * feats
-    )
-    grad_joint = lay.sub_place(product_tn(att_low, grad_joint_out).reshape(D, 3, feats), 2)
     grad_att_in, gain_one, shift_one = norm_back(
         lay.own_sum(product_nt(grad_joint_out, joint_own)), att_normal, att_inv, gain_rows[1]
     )
     grad_one = grad_two + grad_att_in
     earlier = (rows_up_two, rows_down_two, rows_conv, output)
-    moved_joint = lay.scatter(
-        [grad_joint.reshape(D, 3 * D // 2), grad_rel_proj], after=rows_conv
-    )
 
     def scatter_one(grad_down, grad_up, grad_hidden):
         grad_hidden, rows_joint = lax.optimization_barrier((grad_hidden, moved_joint[0]))
         moved_down = lay.scatter([grad_down], after=rows_joint)
-        moved_up = lay.scatter([grad_up], over_planes=True, after=moved_down[0])
+        moved_up = lay.scatter([grad_up, grad_rel_proj], over_planes=True, after=moved_down[0])
         late, _ = lax.optimization_barrier((earlier + (rows_joint,), grad_up))
         return grad_hidden, (moved_down, moved_up, late)
 
@@ -801,9 +813,9 @@
     (summed_up_two,) = lay.collect(rows_up_two, moved_up_two[1])
     (summed_down_two,) = lay.collect(rows_down_two, moved_down_two[1])
     summed_merge, summed_wide, summed_narrow = lay.collect(rows_conv, moved_conv[1])
-    summed_joint, summed_rel = lay.collect(rows_joint, moved_joint[1])
+    (summed_joint,) = lay.collect(rows_joint, moved_joint[1])
     (summed_down_one,) = lay.collect(*moved_down)
-    (summed_up_one,) = lay.collect(*moved_up)
+    summed_up_one, summed_rel = lay.collect(*moved_up)
     summed_up_one = lay.cols_join(summed_up_one, tm)
     summed_up_two = lay.cols_join(summed_up_two, tm)
     summed_joint = lay.cols_join(summed_joint, 3)

time: 1270 us -> 1290 us (1.016)
  waiting for transfers between devices: 355 us -> 384 us
    ppermute x60, waiting for transfers between devices: 180 us -> 197 us  [send(): return lax.ppermute(values, AXES, self.route(target))]
    unnamed x357 -> x361, local copies, waits for them, and re-layouts: 44.6 us -> 45.8 us
  transfers between devices with their start and end apart: 76 -> 76, of which waited for: 37 -> 37; matrix products, arithmetic and copies ran while one was open for 34% -> 33% of each run, Pallas kernels for 15% -> 14%
where the time goes in v3:
time: 1290 us; the launch traced here: 1280 us
  waiting for transfers between devices  384 us (30%)
  matrix products  267 us (21%)
  other arithmetic  184 us (14%)
  Pallas kernels  183 us (14%)
  local copies, waits for them, and re-layouts  152 us (12%)
  starting transfers between devices  93.2 us (7%)
  between operations  18.9 us (1%)
    ppermute x60, waiting for transfers between devices, send(): return lax.ppermute(values, AXES, self.route(target))  197 us
    pallas_call x1, Pallas kernels, attend_back(): pl.pallas_call(functools.partial(attend_back_kernel, slots=slots, rows=ro...  125 us
    dot_general x10, matrix products, product_tn(): lax.dot_general(left, right, (((0,), (0,)), ((), ())), preferred_element_...  92 us
    dot_general x9, matrix products, product(): return jnp.dot(left, right, preferred_element_type=f32)  88.3 us
    dot_general x8, matrix products, product_nt(): lax.dot_general(left, right, (((1,), (1,)), ((), ())), preferred_element_...  86.8 us
    reduce_scatter x6, waiting for transfers between devices, scatter(): mine = lax.psum_scatter(mine, 'tm', scatter_dimension=0, tiled=True)  85.4 us
    all_gather x2, waiting for transfers between devices, gather(): lax.all_gather(packed[None], AXES, axis=0, tiled=True, axis_index_groups=...  67.1 us
    ppermute x60, starting transfers between devices, send(): return lax.ppermute(values, AXES, self.route(target))  66.8 us
  transfers between devices with their start and end apart: 76, of which 37 were waited for; matrix products, arithmetic and copies ran while one was open for 33% of the time, Pallas kernels for 14%

profile of v3, /device:TPU:11, one launch (start us, length us, event | category | flops | bytes accessed | tf_op | source)
XLA Modules:
  0.0 1283.1 jit_solution(15237445760397085752)
XLA Ops:
  44.2 32.8 %collective-permute-done.5 = bf16[2,19,128]{2,1,0:T(8,128)(2,1)S(1)} collective-permute-done((bf16[2,19,128]{2,1,0:T(8,128)(2,1)S(1)}, bf16[2,19,128]{2,1,0:T(8,128)(2,1)S(1)}, u32[]{:S(2)}, u32[]{:S(2)}) %collective-permute-start.5) | collective-permute-done | bytes 9760 | tf_op jit(solution)/shard_map/ppermute | solution.py:291
  79.7 26.9 %collective-permute-done.6 = bf16[4,19,128]{2,1,0:T(8,128)(2,1)S(1)} collective-permute-done((bf16[4,19,128]{2,1,0:T(8,128)(2,1)S(1)}, bf16[4,19,128]{2,1,0:T(8,128)(2,1)S(1)}, u32[]{:S(2)}, u32[]{:S(2)}) %collective-permute-start.6) | collective-permute-done | bytes 19488 | tf_op jit(solution)/shard_map/ppermute | solution.py:291
  115.4 32.8 %fusion = (bf16[4096,512]{1,0:T(8,128)(2,1)}, bf16[4096,512]{1,0:T(8,128)(2,1)}) fusion(f32[512]{0:T(512)S(1)} %multiply_exponential_fusion, f32[4096]{0:T(1024)S(1)} %subtract_convert_fusion.4), kind=kLoop, calls=%fused_computation.9 | loop fusion | flops 6291456 | bytes 8407040 | tf_op jit(solution)/shard_map/convert.39
  156.2 45.1 %all-gather.5.cloned.1.call-done = bf16[6144,1024]{1,0:T(8,128)(2,1)} async-done(((bf16[384,1024]{1,0:T(8,128)(2,1)}), bf16[6144,1024]{1,0:T(8,128)(2,1)}) %all-gather.5.cloned.1.call-update) | async-done | bytes 12582928 | tf_op jit(solution)/shard_map/all_gather | solution.py:424
  211.3 19.7 %multiply_convert_fusion.3 = (bf16[2048,2048]{1,0:T(8,128)(2,1)}, f32[2048,2048]{1,0:T(8,128)}) fusion(bf16[1024,2048]{1,0:T(8,128)(2,1)S(1)} %bitcast.400, bf16[1024,1024]{1,0:T(8,128)(2,1)} %collective-permute-done.7, bf16[1024,1024]{1,0:T(8,128)(2,1)} %fusion.39), kind=kOutput, calls=%fused_computation.5 | convolution fusion | flops 8619294720 | bytes 33554432 | tf_op jit(solution)/shard_map/dot_general | solution.py:25
  231.0 11.7 fusion.154
  282.5 58.5 %attend.1 = (bf16[2,1024,512]{2,1,0:T(8,128)(2,1)}, f32[4,2048,1]{2,1,0:T(8,128)}) custom-call(s32[1]{0:T(128)} %bitcast.own_ref, bf16[2,1024,1536]{2,1,0:T(8,128)(2,1)} %bitcast.514, bf16[2,1024,1536]{2,1,0:T(8,128)(2,1)} %bitcast.515, bf16[2,1024,1536]{2,1,0:T(8,128)(2,1)} %bitcast.516, bf16[4096,512]{1,0:T(8,128)(2,1)} %convolution_convert_fusion.1.rel_ref, ...), custom_call_target="tpu_custom_call" | custom-call | flops 42949672960 | bytes 20971520 | tf_op jit(solution)/shard_map/attend/pallas_call | solution.py:179
  342.8 22.0 %all-gather.7.cloned.1.call-done = bf16[6656,1024]{1,0:T(8,128)(2,1)} async-done(((bf16[416,1024]{1,0:T(8,128)(2,1)}), bf16[6656,1024]{1,0:T(8,128)(2,1)}) %all-gather.7.cloned.1.call-update) | async-done | bytes 13631504 | tf_op jit(solution)/shard_map/all_gather | solution.py:424
  422.9 13.2 %collective-permute-done.14 = bf16[1,256,1024]{2,1,0:T(8,128)(2,1)S(1)} collective-permute-done((bf16[1,256,1024]{2,1,0:T(8,128)(2,1)S(1)}, bf16[1,256,1024]{2,1,0:T(8,128)(2,1)S(1)}, u32[]{:S(2)}, u32[]{:S(2)}) %collective-permute-start.14) | collective-permute-done | bytes 524320 | tf_op jit(solution)/shard_map/ppermute | solution.py:291
  470.4 18.7 %multiply_convert_fusion.2 = (bf16[2048,2048]{1,0:T(8,128)(2,1)}, f32[2048,2048]{1,0:T(8,128)}) fusion(bf16[1024,2048]{1,0:T(8,128)(2,1)S(1)} %bitcast.405, bf16[1024,1024]{1,0:T(8,128)(2,1)} %copy-done.150, bf16[1024,1024]{1,0:T(8,128)(2,1)S(1)} %add_convert_fusion.2), kind=kOutput, calls=%fused_computation.3 | convolution fusion | flops 8619294720 | bytes 33554432 | tf_op jit(solution)/shard_map/dot_general | solution.py:25
  529.4 20.6 %multiply_convert_fusion.1 = bf16[2048,2048]{1,0:T(8,128)(2,1)} fusion(f32[2048,2048]{1,0:T(8,128)} %get-tuple-element.354, bf16[2048,1024]{1,0:T(8,128)(2,1)} %pad_maximum_fusion.11, bf16[2048,1024]{1,0:T(8,128)(2,1)} %bitcast.408), kind=kOutput, calls=%fused_computation.2 | convolution fusion | flops 8627683328 | bytes 33554432 | tf_op jit(solution)/shard_map/dot_general | solution.py:29
  550.0 14.7 %convolution_convert_fusion.4 = bf16[1024,2048]{1,0:T(8,128)(2,1)} fusion(bf16[2048,2048]{1,0:T(8,128)(2,1)} %multiply_convert_fusion.1, bf16[1024,1024]{1,0:T(8,128)(2,1)} %copy-done.150, bf16[1024,1024]{1,0:T(8,128)(2,1)} %copy-done.48), kind=kOutput, calls=%fused_computation.152 | convolution fusion | flops 8600420352 | bytes 16777216 | tf_op jit(solution)/shard_map/dot_general | solution.py:33
  564.7 11.5 fusion.158
  724.3 125.0 %attend_back.1 = (bf16[2,1024,512]{2,1,0:T(8,128)(2,1)}, bf16[2,1024,512]{2,1,0:T(8,128)(2,1)}, bf16[2,1024,512]{2,1,0:T(8,128)(2,1)}, f32[4096,512]{1,0:T(8,128)}, f32[4,2,128]{2,1,0:T(2,128)}) custom-call(s32[1]{0:T(128)} %bitcast.own_ref, bf16[2,1024,1536]{2,1,0:T(8,128)(2,1)} %bitcast.517, bf16[2,1024,1536]{2,1,0:T(8,128)(2,1)} %bitcast.518, ...), custom_call_target="tpu_custom_call" | custom-call | flops 107374182400 | bytes 41943040 | tf_op jit(solution)/shard_map/attend_back/pallas_call | solution.py:208
  849.3 56.1 %reduce-scatter.11.cloned.1.call-done = bf16[1,2,160,1024]{3,2,1,0:T(8,128)(2,1)} async-done(((bf16[8,2,160,1024]{3,2,1,0:T(8,128)(2,1)}), bf16[1,2,160,1024]{3,2,1,0:T(8,128)(2,1)}) %reduce-scatter.11.cloned.1.call-update) | async-done | bytes 655376 | tf_op jit(solution)/shard_map/reduce_scatter | solution.py:445
  949.5 11.3 add_convert_fusion.5
  961.0 13.8 %convolution_convert_fusion.5 = bf16[2048,1024]{1,0:T(8,128)(2,1)} fusion(bf16[2048,2048]{1,0:T(8,128)(2,1)} %get-tuple-element.349, bf16[1024,1024]{1,0:T(8,128)(2,1)} %collective-permute-done.39, bf16[1024,1024]{1,0:T(8,128)(2,1)S(1)} %get-tuple-element.188), kind=kOutput, calls=%fused_computation.153 | convolution fusion | flops 8600420352 | bytes 16777216 | tf_op jit(solution)/shard_map/dot_general | solution.py:33
  979.1 19.9 %multiply_convert_fusion = bf16[2048,2048]{1,0:T(8,128)(2,1)} fusion(f32[2048,2048]{1,0:T(8,128)} %get-tuple-element.350, bf16[2048,1024]{1,0:T(8,128)(2,1)} %pad_maximum_fusion.17, bf16[2048,1024]{1,0:T(8,128)(2,1)S(1)} %bitcast.403), kind=kOutput, calls=%fused_computation.1 | convolution fusion | flops 8627683328 | bytes 33554432 | tf_op jit(solution)/shard_map/dot_general | solution.py:29
  999.0 13.0 %convolution_convert_fusion.3 = bf16[1024,2048]{1,0:T(8,128)(2,1)S(1)} fusion(bf16[2048,2048]{1,0:T(8,128)(2,1)} %multiply_convert_fusion, bf16[1024,1024]{1,0:T(8,128)(2,1)} %collective-permute-done.7, bf16[1024,1024]{1,0:T(8,128)(2,1)} %fusion.39), kind=kOutput, calls=%fused_computation.151 | convolution fusion | flops 8600420352 | bytes 16777216 | tf_op jit(solution)/shard_map/dot_general | solution.py:33
  1018.9 29.3 %reduce-scatter.13.cloned.1.call-done = bf16[1,2,128,1024]{3,2,1,0:T(8,128)(2,1)} async-done(((bf16[8,2,128,1024]{3,2,1,0:T(8,128)(2,1)}), bf16[1,2,128,1024]{3,2,1,0:T(8,128)(2,1)}) %reduce-scatter.13.cloned.1.call-update) | async-done | bytes 524304 | tf_op jit(solution)/shard_map/reduce_scatter | solution.py:445
  1050.9 33.7 %collective-permute-done.45 = bf16[8,192,1024]{2,1,0:T(8,128)(2,1)} collective-permute-done((bf16[8,192,1024]{2,1,0:T(8,128)(2,1)}, bf16[8,192,1024]{2,1,0:T(8,128)(2,1)}, u32[]{:S(2)}, u32[]{:S(2)}) %collective-permute-start.45) | collective-permute-done | bytes 3145760 | tf_op jit(solution)/shard_map/ppermute | solution.py:291
  1088.6 12.6 fusion.160
  1113.3 11.3 collective-permute-done.57
  1245.4 13.9 %collective-permute-done.43 = bf16[1,256,1024]{2,1,0:T(8,128)(2,1)} collective-permute-done((bf16[1,256,1024]{2,1,0:T(8,128)(2,1)}, bf16[1,256,1024]{2,1,0:T(8,128)(2,1)}, u32[]{:S(2)}, u32[]{:S(2)}) %collective-permute-start.43) | collective-permute-done | bytes 524320 | tf_op jit(solution)/shard_map/ppermute | solution.py:331
  (839 shorter events, 596.1 us)
Async XLA Ops:
  7.2 194.1 %all-gather.5.cloned.1.call-start = ((), (), s32[]{:S(2)}) async-start(), calls=%async_computation.12 | async-start | bytes 13369344 | tf_op jit(solution)/shard_map/all_gather | solution.py:424
  14.0 350.8 %all-gather.7.cloned.1.call-start = ((), (), s32[]{:S(2)}) async-start(), calls=%async_computation.13 | async-start | bytes 14483456 | tf_op jit(solution)/shard_map/all_gather | solution.py:424
  22.6 826.7 %reduce-scatter.7.cloned.1.call-start = ((), (), s32[]{:S(2)}) async-start(), calls=%async_computation.6 | async-start | bytes 4718592 | tf_op jit(solution)/shard_map/reduce_scatter | solution.py:445
  23.9 84.6 %collective-permute-start = (bf16[1,256,1024]{2,1,0:T(8,128)(2,1)S(1)}, bf16[1,256,1024]{2,1,0:T(8,128)(2,1)}, u32[]{:S(2)}, u32[]{:S(2)}) collective-permute-start(bf16[1,256,1024]{2,1,0:T(8,128)(2,1)S(1)} %get-tuple-element.276), channel_id=1, source_target_pairs={{0,0},{1,2},{2,4},{3,6},{4,8},{5,10},{6,12},{7,14},{8,1},{9,3},{10... | collective-permute-start | bytes 1572872 | tf_op jit(solution)/shard_map/ppermute | solution.py:291
  28.7 81.3 %collective-permute-start.1 = (bf16[1,256,1024]{2,1,0:T(8,128)(2,1)}, bf16[1,256,1024]{2,1,0:T(8,128)(2,1)}, u32[]{:S(2)}, u32[]{:S(2)}) collective-permute-start(bf16[1,256,1024]{2,1,0:T(8,128)(2,1)} %get-tuple-element.275), channel_id=1, source_target_pairs={{0,2},{1,4},{2,6},{3,0},{4,10},{5,12},{6,14},{7,8},{8,3},{9,5},{10... | collective-permute-start | bytes 1572872 | tf_op jit(solution)/shard_map/ppermute | solution.py:291
  30.6 80.5 %collective-permute-start.2 = (bf16[1,256,1024]{2,1,0:T(8,128)(2,1)}, bf16[1,256,1024]{2,1,0:T(8,128)(2,1)S(1)}, u32[]{:S(2)}, u32[]{:S(2)}) collective-permute-start(bf16[1,256,1024]{2,1,0:T(8,128)(2,1)} %get-tuple-element.274), channel_id=1, source_target_pairs={{0,4},{1,6},{2,0},{3,2},{4,12},{5,14},{6,8},{7,10},{8,5},{9,7},{10... | collective-permute-start | bytes 1572872 | tf_op jit(solution)/shard_map/ppermute | solution.py:291
  31.0 80.1 %collective-permute-start.3 = (bf16[1,256,1024]{2,1,0:T(8,128)(2,1)}, bf16[1,256,1024]{2,1,0:T(8,128)(2,1)S(1)}, u32[]{:S(2)}, u32[]{:S(2)}) collective-permute-start(bf16[1,256,1024]{2,1,0:T(8,128)(2,1)} %get-tuple-element.273), channel_id=1, source_target_pairs={{0,6},{1,0},{2,2},{3,4},{4,14},{5,8},{6,10},{7,12},{8,7},{9,1},{10... | collective-permute-start | bytes 1572872 | tf_op jit(solution)/shard_map/ppermute | solution.py:291
  114.5 96.8 %collective-permute-start.7 = (bf16[1024,1024]{1,0:T(8,128)(2,1)}, bf16[1024,1024]{1,0:T(8,128)(2,1)}, u32[]{:S(2)}, u32[]{:S(2)}) collective-permute-start(bf16[1024,1024]{1,0:T(8,128)(2,1)} %fusion.39), channel_id=1, source_target_pairs={{0,8},{1,9},{2,10},{3,11},{4,12},{5,13},{6,14},{7,15},{8,0},{9,1},... | collective-permute-start | bytes 6291464 | tf_op jit(solution)/shard_map/ppermute | solution.py:291
  384.4 38.5 %collective-permute-start.13 = (bf16[1,256,1024]{2,1,0:T(8,128)(2,1)S(1)}, bf16[1,256,1024]{2,1,0:T(8,128)(2,1)S(1)}, u32[]{:S(2)}, u32[]{:S(2)}) collective-permute-start(bf16[1,256,1024]{2,1,0:T(8,128)(2,1)S(1)} %get-tuple-element.268), channel_id=1, source_target_pairs={{0,0},{1,2},{2,4},{3,6},{4,8},{5,10},{6,12},{7,14},{8,1},{9,3},{10... | collective-permute-start | bytes 1572872 | tf_op jit(solution)/shard_map/ppermute | solution.py:291
  388.3 47.8 %collective-permute-start.14 = (bf16[1,256,1024]{2,1,0:T(8,128)(2,1)S(1)}, bf16[1,256,1024]{2,1,0:T(8,128)(2,1)S(1)}, u32[]{:S(2)}, u32[]{:S(2)}) collective-permute-start(bf16[1,256,1024]{2,1,0:T(8,128)(2,1)S(1)} %get-tuple-element.267), channel_id=1, source_target_pairs={{0,2},{1,4},{2,6},{3,0},{4,10},{5,12},{6,14},{7,8},{8,3},{9,5},{10... | collective-permute-start | bytes 1572872 | tf_op jit(solution)/shard_map/ppermute | solution.py:291
  390.2 45.9 %collective-permute-start.15 = (bf16[1,256,1024]{2,1,0:T(8,128)(2,1)S(1)}, bf16[1,256,1024]{2,1,0:T(8,128)(2,1)}, u32[]{:S(2)}, u32[]{:S(2)}) collective-permute-start(bf16[1,256,1024]{2,1,0:T(8,128)(2,1)S(1)} %get-tuple-element.266), channel_id=1, source_target_pairs={{0,4},{1,6},{2,0},{3,2},{4,12},{5,14},{6,8},{7,10},{8,5},{9,7},{10... | collective-permute-start | bytes 1572872 | tf_op jit(solution)/shard_map/ppermute | solution.py:291
  390.7 45.4 %collective-permute-start.16 = (bf16[1,256,1024]{2,1,0:T(8,128)(2,1)S(1)}, bf16[1,256,1024]{2,1,0:T(8,128)(2,1)}, u32[]{:S(2)}, u32[]{:S(2)}) collective-permute-start(bf16[1,256,1024]{2,1,0:T(8,128)(2,1)S(1)} %get-tuple-element.265), channel_id=1, source_target_pairs={{0,6},{1,0},{2,2},{3,4},{4,14},{5,8},{6,10},{7,12},{8,7},{9,1},{10... | collective-permute-start | bytes 1572872 | tf_op jit(solution)/shard_map/ppermute | solution.py:291
  595.1 254.2 %reduce-scatter.9.cloned.1.call-start = ((), (), s32[]{:S(2)}) async-start(), calls=%async_computation.7 | async-start | bytes 4718592 | tf_op jit(solution)/shard_map/reduce_scatter | solution.py:445
  651.0 254.4 %reduce-scatter.11.cloned.1.call-start = ((), (), s32[]{:S(2)}) async-start(), calls=%async_computation.8 | async-start | bytes 5898240 | tf_op jit(solution)/shard_map/reduce_scatter | solution.py:445
  706.1 342.1 %reduce-scatter.13.cloned.1.call-start = ((), (), s32[]{:S(2)}) async-start(), calls=%async_computation.9 | async-start | bytes 4718592 | tf_op jit(solution)/shard_map/reduce_scatter | solution.py:445
  711.9 137.3 %collective-permute-start.34 = (bf16[1,256,1024]{2,1,0:T(8,128)(2,1)S(1)}, bf16[1,256,1024]{2,1,0:T(8,128)(2,1)}, u32[]{:S(2)}, u32[]{:S(2)}) collective-permute-start(bf16[1,256,1024]{2,1,0:T(8,128)(2,1)S(1)} %get-tuple-element.252), channel_id=1, source_target_pairs={{0,0},{2,1},{4,2},{6,3},{8,4},{10,5},{12,6},{14,7},{1,8},{3,9},{5,... | collective-permute-start | bytes 1572872 | tf_op jit(solution)/shard_map/ppermute | solution.py:331
  714.6 134.7 %collective-permute-start.35 = (bf16[1,256,1024]{2,1,0:T(8,128)(2,1)S(1)}, bf16[1,256,1024]{2,1,0:T(8,128)(2,1)}, u32[]{:S(2)}, u32[]{:S(2)}) collective-permute-start(bf16[1,256,1024]{2,1,0:T(8,128)(2,1)S(1)} %get-tuple-element.251), channel_id=1, source_target_pairs={{2,0},{4,1},{6,2},{0,3},{10,4},{12,5},{14,6},{8,7},{3,8},{5,9},{7,... | collective-permute-start | bytes 1572872 | tf_op jit(solution)/shard_map/ppermute | solution.py:331
  719.5 129.8 %collective-permute-start.36 = (bf16[1,256,1024]{2,1,0:T(8,128)(2,1)S(1)}, bf16[1,256,1024]{2,1,0:T(8,128)(2,1)}, u32[]{:S(2)}, u32[]{:S(2)}) collective-permute-start(bf16[1,256,1024]{2,1,0:T(8,128)(2,1)S(1)} %get-tuple-element.250), channel_id=1, source_target_pairs={{4,0},{6,1},{0,2},{2,3},{12,4},{14,5},{8,6},{10,7},{5,8},{7,9},{1,... | collective-permute-start | bytes 1572872 | tf_op jit(solution)/shard_map/ppermute | solution.py:331
  720.2 129.1 %collective-permute-start.37 = (bf16[1,256,1024]{2,1,0:T(8,128)(2,1)S(1)}, bf16[1,256,1024]{2,1,0:T(8,128)(2,1)}, u32[]{:S(2)}, u32[]{:S(2)}) collective-permute-start(bf16[1,256,1024]{2,1,0:T(8,128)(2,1)S(1)} %get-tuple-element.249), channel_id=1, source_target_pairs={{6,0},{0,1},{2,2},{4,3},{14,4},{8,5},{10,6},{12,7},{7,8},{1,9},{3,... | collective-permute-start | bytes 1572872 | tf_op jit(solution)/shard_map/ppermute | solution.py:331
  960.9 187.9 %reduce-scatter.15.cloned.1.call-start = ((), (), s32[]{:S(2)}) async-start(), calls=%async_computation.10 | async-start | bytes 4718592 | tf_op jit(solution)/shard_map/reduce_scatter | solution.py:445
  1014.6 70.0 %collective-permute-start.45 = (bf16[8,192,1024]{2,1,0:T(8,128)(2,1)}, bf16[8,192,1024]{2,1,0:T(8,128)(2,1)}, u32[]{:S(2)}, u32[]{:S(2)}) collective-permute-start(bf16[8,192,1024]{2,1,0:T(8,128)(2,1)} %fusion.47), channel_id=1, source_target_pairs={{0,16},{1,17},{2,18},{3,19},{4,20},{5,21},{6,22},{7,23},{8,24},{9,... | collective-permute-start | bytes 9437192 | tf_op jit(solution)/shard_map/ppermute | solution.py:291
  1048.3 185.1 %reduce-scatter.17.cloned.1.call-start = ((), (), s32[]{:S(2)}) async-start(), calls=%async_computation.11 | async-start | bytes 3538944 | tf_op jit(solution)/shard_map/reduce_scatter | solution.py:445
  1103.0 74.3 %collective-permute-start.40 = (bf16[1024,1024]{1,0:T(8,128)(2,1)}, bf16[1024,1024]{1,0:T(8,128)(2,1)}, u32[]{:S(2)}, u32[]{:S(2)}) collective-permute-start(bf16[1024,1024]{1,0:T(8,128)(2,1)} %slice.831), channel_id=1, source_target_pairs={{0,8},{1,9},{2,10},{3,11},{4,12},{5,13},{6,14},{7,15},{8,0},{9,1},... | collective-permute-start | bytes 6291464 | tf_op jit(solution)/shard_map/ppermute | solution.py:291
  1221.7 44.8 %collective-permute-start.44 = (bf16[1,256,1024]{2,1,0:T(8,128)(2,1)}, bf16[1,256,1024]{2,1,0:T(8,128)(2,1)S(1)}, u32[]{:S(2)}, u32[]{:S(2)}) collective-permute-start(bf16[1,256,1024]{2,1,0:T(8,128)(2,1)} %get-tuple-element.245), channel_id=1, source_target_pairs={{6,0},{0,1},{2,2},{4,3},{14,4},{8,5},{10,6},{12,7},{7,8},{1,9},{3,... | collective-permute-start | bytes 1572872 | tf_op jit(solution)/shard_map/ppermute | solution.py:331
  (217 other events, 2649.9 us)
Sparse Core Ops, SparseCore 0:
  14.1 187.0 all-gather.4
  204.7 160.0 all-gather.6
  595.2 89.1 reduce-scatter.6
  688.4 111.3 reduce-scatter.8
  803.2 102.1 reduce-scatter.10
  961.1 87.1 reduce-scatter.12
  1052.3 87.6 reduce-scatter.14
  1149.0 76.9 reduce-scatter.16
